TPU v7x, 128 devices: a whole 4x4x4 slice. The times are simulated.
128 devices in a mesh: tg: 2 (over core), pw: 64 (over y, x, z).
Axes of the slice: x: 4, y: 4, z: 4, core: 2. Of those that a mesh axis runs over, the one named last changes fastest.
Arguments:
- coeffs: float32 [2, 32768, 256], P(None, ('tg', 'pw')), may hold values from -6 to 6
- g_place: int32 [32768], P(('tg', 'pw')), may hold values from 0 to 2047, as said below
- stick_column: int32 [2048], P(('tg', 'pw')), may hold values from 0 to 16383, as said below
- potential: float32 [128, 128, 128], P(None, None, ('tg', 'pw')), may hold values from -1 to 3
Outputs:
- hpsi: float32 [2, 32768, 256], P(None, ('tg', 'pw'))
Inputs may be any that keep to these rules, and one draw needn't show every extreme that they name: g_place[g] = s * 128 + z: s is a stick slot of the owner g // 256, z a frequency within 32 of zero taken modulo 128; no two plane waves of one owner share s and z; each owner uses its slots 0 up to some count between 4 and 16, every one of them, and some owner uses all 16. `stick_column`: all stick slots name different columns x * 128 + y; with x and y read as signed frequencies (taken modulo 128), x * x + y * y <= 32 ** 2.
All inputs are finite; a program needn't handle non-finite values.
Results may differ from a plain program's by a relative error of at most 0.009.
Values may be sent and summed in bfloat16 or wider, within the bound.
No kernel may reach another device: no remote copies, remote signals or barrier semaphores. Data moves between devices by JAX's collectives and lax.ppermute only.
A program may use at most 128 MiB of HBM per device.

v0:
```python
import numpy as np
import jax
import jax.numpy as jnp
from jax import lax
from jax.experimental import pallas as pl
from jax.experimental.pallas import tpu as pltpu
from jax.sharding import Mesh
from jax.sharding import PartitionSpec as P

NR = 128
HALF = 32
BOX = 72
PAIRS = 33
SLOT = 16
LANES = 128
TG_PW = ("tg", "pw_0", "pw_1", "pw_2")
BF = jnp.bfloat16
F32 = jnp.float32
VMEM = pl.BlockSpec(memory_space=pltpu.VMEM)
SMEM = pl.BlockSpec(memory_space=pltpu.SMEM)


def complex_table(rows, cols, sign, keep_rows, keep_cols):
    angle = 2.0 * np.pi / NR * (np.outer(rows, cols) % NR)
    keep = keep_rows[:, None] * keep_cols[None, :]
    c = np.cos(angle) * keep
    s = sign * np.sin(angle) * keep
    return np.stack([np.stack([c, -s], 1), np.stack([s, c], 1)]).astype(np.float32)


def tables():
    full = np.arange(NR)
    box = np.arange(BOX) - HALF
    keep_box = (np.arange(BOX) <= 2 * HALF).astype(np.float32)
    keep_all = np.ones(NR, np.float32)
    ahead = complex_table(full, box, 1.0, keep_all, keep_box)
    behind = complex_table(box, full, -1.0, keep_box, keep_all)
    wide, tall = 2 * NR, 2 * BOX
    ahead_y = ahead.transpose(1, 0, 3, 2).reshape(wide, tall)
    ahead_x = ahead.reshape(wide, tall)
    behind_x = behind.reshape(tall, wide)
    behind_y = behind.transpose(1, 0, 3, 2).reshape(tall, wide)
    return [jnp.asarray(t, BF) for t in (ahead_y, ahead_x, behind_x, behind_y)]


def spread_kernel(c_ref, place_ref, info_ref, e_ref, a_ref, b_ref, t_ref):
    place = place_ref[...]
    row = (place >> 7) * BOX + ((place + HALF) & (NR - 1))
    at = lax.broadcasted_iota(jnp.int32, (SLOT * BOX, place.shape[1]), 0)
    select = jnp.where(at == row, 1.0, 0.0).astype(BF)
    parts = [
        jnp.dot(select, c_ref[p].astype(BF), preferred_element_type=F32) for p in range(2)
    ]
    for s in range(SLOT):
        x = jnp.concatenate([parts[p][s * BOX : (s + 1) * BOX] for p in range(2)], axis=0)
        m = jnp.dot(e_ref[...], x.astype(BF), preferred_element_type=F32)
        for h in range(2):
            for p in range(2):
                t_ref[h, pl.ds(2 * s + p, NR, stride=2 * SLOT), :] = m[
                    p * NR : (p + 1) * NR, h * LANES : (h + 1) * LANES
                ]
    info = jnp.broadcast_to(info_ref[...], (8, LANES)).astype(F32).astype(BF)

    @pl.loop(0, NR // 4)
    def _(i):
        for u in range(4):
            k = i * 4 + u
            rows = pl.ds(pl.multiple_of(k * 2 * SLOT, 2 * SLOT), 2 * SLOT)
            a_ref[k, 0 : 2 * SLOT, :] = t_ref[0, rows, :].astype(BF)
            a_ref[k, 2 * SLOT : 2 * SLOT + 8, :] = info
            b_ref[k] = t_ref[1, rows, :].astype(BF)


def spread(coeffs, place, info, ahead_z):
    return pl.pallas_call(
        spread_kernel,
        out_shape=(
            jax.ShapeDtypeStruct((NR, 2 * SLOT + 8, LANES), BF),
            jax.ShapeDtypeStruct((NR, 2 * SLOT, LANES), BF),
        ),
        in_specs=[VMEM] * 4,
        out_specs=(VMEM, VMEM),
        scratch_shapes=[pltpu.VMEM((2, NR * 2 * SLOT, LANES), F32)],
        compiler_params=pltpu.CompilerParams(vmem_limit_bytes=40 << 20),
        cost_estimate=pl.CostEstimate(
            flops=2 * (1152 * 256 * 512 + 4096 * 256 * 256), bytes_accessed=3 << 20, transcendentals=0
        ),
        name="spread",
    )(coeffs, place, info, ahead_z)


def plane_kernel(
    cell_ref, r_ref, v_ref, ey_ref, ex_ref, ix_ref, iy_ref, o_ref, f_ref, g_ref, s_ref, w_ref
):
    sticks = f_ref.shape[0] // 2
    owners = r_ref.shape[0]
    per = 2 * SLOT
    two = 2 * BOX
    blank = jnp.zeros((two, LANES), F32)

    @pl.loop(0, 2 * PAIRS)
    def _(x):
        g_ref[pl.ds(pl.multiple_of(x * two, 8), two), :] = blank

    @pl.loop(0, NR // 8)
    def _(i):
        for u in range(16):
            s_ref[pl.ds(pl.multiple_of((i * 16 + u) * BOX + 64, 8), 8), :] = blank[:8]

    @pl.loop(0, owners // 8)
    def _(i):
        for u in range(8):
            o = i * 8 + u
            f_ref[pl.ds(pl.multiple_of(o * per, per), per), :] = r_ref[o, 0:per, :].astype(F32)

    step = 32

    @pl.loop(0, sticks // step)
    def _(i):
        for u in range(step):
            c = cell_ref[i * step + u]
            g_ref[pl.ds(2 * c, 2), :] = f_ref[
                pl.ds(pl.multiple_of(i * 2 * step, 2 * step) + 2 * u, 2), :
            ]

    turn = 11

    @pl.loop(0, PAIRS // turn)
    def _(i):
        xs = []
        for u in range(turn):
            r0 = (i * turn + u) * 2 * two
            a = g_ref[pl.ds(pl.multiple_of(r0, 8), two), :].astype(BF)
            b = g_ref[pl.ds(pl.multiple_of(r0 + two, 8), two), :].astype(BF)
            xs.append(jnp.concatenate([a, b], axis=1))
        for u in range(turn):
            m = jnp.dot(ey_ref[...], xs[u], preferred_element_type=F32)
            x0 = 2 * (i * turn + u)
            s_ref[pl.ds(x0, 2 * NR, stride=BOX), :] = m[:, :LANES]
            s_ref[pl.ds(x0 + 1, 2 * NR, stride=BOX), :] = m[:, LANES:]

    lane = lax.broadcasted_iota(jnp.int32, (NR, NR), 1)
    v = v_ref[...]
    batch = 16

    @pl.loop(0, NR // 2 // batch)
    def _(i):
        xs = []
        for u in range(batch):
            r0 = (i * batch + u) * 2 * two
            a = s_ref[pl.ds(pl.multiple_of(r0, 8), two), :].astype(BF)
            b = s_ref[pl.ds(pl.multiple_of(r0 + two, 8), two), :].astype(BF)
            xs.append(jnp.concatenate([a, b], axis=1))
        for u in range(batch):
            psi = jnp.dot(ex_ref[...], xs[u], preferred_element_type=F32)
            q = 2 * (i * batch + u)
            vs = []
            for t in range(2):
                column = jnp.sum(jnp.where(lane == q + t, v, 0.0), axis=1, keepdims=True)
                vs.append(jnp.broadcast_to(column, (NR, LANES)))
            vv = jnp.concatenate(vs, axis=1)
            w_ref[u] = (psi * jnp.concatenate([vv, vv], axis=0)).astype(BF)
        for u in range(batch):
            h = jnp.dot(ix_ref[...], w_ref[u], preferred_element_type=F32)
            r0 = (i * batch + u) * 2 * two
            s_ref[pl.ds(pl.multiple_of(r0, 8), two), :] = h[:, :LANES]
            s_ref[pl.ds(pl.multiple_of(r0 + two, 8), two), :] = h[:, LANES:]

    @pl.loop(0, PAIRS // turn)
    def _(i):
        xs = []
        for u in range(turn):
            x0 = 2 * (i * turn + u)
            a = s_ref[pl.ds(x0, 2 * NR, stride=BOX), :].astype(BF)
            b = s_ref[pl.ds(x0 + 1, 2 * NR, stride=BOX), :].astype(BF)
            xs.append(jnp.concatenate([a, b], axis=1))
        for u in range(turn):
            m = jnp.dot(iy_ref[...], xs[u], preferred_element_type=F32)
            r0 = (i * turn + u) * 2 * two
            g_ref[pl.ds(pl.multiple_of(r0, 8), two), :] = m[:, :LANES]
            g_ref[pl.ds(pl.multiple_of(r0 + two, 8), two), :] = m[:, LANES:]

    @pl.loop(0, sticks // step)
    def _(i):
        for u in range(step):
            c = cell_ref[i * step + u]
            f_ref[pl.ds(pl.multiple_of(i * 2 * step, 2 * step) + 2 * u, 2), :] = g_ref[
                pl.ds(2 * c, 2), :
            ]

    @pl.loop(0, owners // 8)
    def _(i):
        for u in range(8):
            o = i * 8 + u
            o_ref[o] = f_ref[pl.ds(pl.multiple_of(o * per, per), per), :].astype(BF)


def plane_pass(cells, received, volume, tabs):
    owners = received.shape[0]
    return pl.pallas_call(
        plane_kernel,
        out_shape=jax.ShapeDtypeStruct((owners, 2 * SLOT, LANES), BF),
        in_specs=[SMEM] + [VMEM] * 6,
        out_specs=VMEM,
        scratch_shapes=[
            pltpu.VMEM((owners * 2 * SLOT, LANES), F32),
            pltpu.VMEM((2 * PAIRS * 2 * BOX, LANES), F32),
            pltpu.VMEM((2 * NR * BOX, LANES), F32),
            pltpu.VMEM((16, 2 * NR, 2 * LANES), BF),
        ],
        compiler_params=pltpu.CompilerParams(vmem_limit_bytes=40 << 20),
        cost_estimate=pl.CostEstimate(
            flops=2 * 38500 * 256 * 256, bytes_accessed=3 << 20, transcendentals=0
        ),
        name="plane",
    )(cells, received, volume, *tabs)


def finish_kernel(r_ref, place_ref, i_ref, *rest):
    o_ref, t_ref, sp_ref = rest[-3:]
    per = 2 * SLOT

    @pl.loop(0, NR // 8)
    def _(i):
        for u in range(8):
            k = i * 8 + u
            t_ref[pl.ds(pl.multiple_of(k * per, per), per), :] = r_ref[k].astype(F32)

    for j in range(SLOT // 2):
        pair = [
            jnp.concatenate(
                [t_ref[pl.ds(2 * (2 * j + q) + p, NR, stride=per), :] for p in range(2)], axis=0
            )
            for q in range(2)
        ]
        x = jnp.concatenate(pair, axis=1).astype(BF)
        m = jnp.dot(i_ref[...], x, preferred_element_type=F32)
        for q in range(2):
            rows = pl.ds((2 * j + q) * BOX, BOX)
            for p in range(2):
                sp_ref[rows, p * LANES : (p + 1) * LANES] = m[
                    p * BOX : (p + 1) * BOX, q * LANES : (q + 1) * LANES
                ]
    place = place_ref[...]
    row = (place >> 7) * BOX + ((place + HALF) & (NR - 1))
    at = lax.broadcasted_iota(jnp.int32, (place.shape[0], SLOT * BOX), 1)
    select = jnp.where(at == row, 1.0 / NR**3, 0.0).astype(BF)
    out = jnp.dot(select, sp_ref[...].astype(BF), preferred_element_type=F32)
    for p in range(2):
        o_ref[p] = out[:, p * LANES : (p + 1) * LANES]


def finish(returned, place, behind_z, half, into=None):
    count = place.shape[0]
    extra = [] if into is None else [into]
    return pl.pallas_call(
        finish_kernel,
        grid=(1,),
        out_shape=jax.ShapeDtypeStruct((2, count, 2 * LANES), F32),
        in_specs=[VMEM] * 3 + [pl.BlockSpec(memory_space=pl.ANY)] * len(extra),
        out_specs=pl.BlockSpec((2, count, LANES), lambda i: (0, 0, half)),
        scratch_shapes=[
            pltpu.VMEM((NR * 2 * SLOT, LANES), F32),
            pltpu.VMEM((SLOT * BOX, 2 * LANES), F32),
        ],
        input_output_aliases={} if into is None else {3: 0},
        compiler_params=pltpu.CompilerParams(vmem_limit_bytes=24 << 20),
        cost_estimate=pl.CostEstimate(
            flops=2 * (1152 + 1280) * 256 * 256, bytes_accessed=2 << 20, transcendentals=0
        ),
        name="finish",
    )(returned, place, behind_z, *extra)


def exchange(value):
    return lax.all_to_all(value, TG_PW, split_axis=0, concat_axis=0, tiled=True)


def body(coeffs, g_place, stick_column, potential):
    tabs = tables()
    ahead_z, behind_z = tabs[1], tabs[2]
    x_box = ((stick_column >> 7) + HALF) & (NR - 1)
    y_box = (stick_column + HALF) & (NR - 1)
    info = jnp.pad(jnp.concatenate([x_box, y_box]), (0, LANES - 2 * SLOT)).reshape(1, LANES)
    sent_a, sent_b = spread(coeffs, g_place.reshape(1, -1), info, ahead_z)
    got_a = exchange(sent_a)
    got_b = exchange(sent_b)
    column = got_a[:, 2 * SLOT, : 2 * SLOT].astype(F32).astype(jnp.int32)
    cells = (column[:, :SLOT] * BOX + column[:, SLOT:]).reshape(-1)
    volume = potential.reshape(NR, NR)
    done_a = plane_pass(cells, got_a, volume, tabs)
    back_a = exchange(done_a)
    done_b = plane_pass(cells, got_b, volume, tabs)
    back_b = exchange(done_b)
    place = g_place.reshape(-1, 1)
    out = finish(back_a, place, behind_z, 0)
    return finish(back_b, place, behind_z, 1, out)


def solution(mesh):
    torus = Mesh(mesh.devices.reshape(mesh.shape["tg"], 4, 4, 4), ("tg", "pw_0", "pw_1", "pw_2"))
    return jax.shard_map(
        body,
        mesh=torus,
        in_specs=(P(None, TG_PW, None), P(TG_PW), P(TG_PW), P(None, None, TG_PW)),
        out_specs=P(None, TG_PW, None),
        check_vma=False,
    )
```

profile of v0, /device:TPU:1, one launch (start us, length us, event | category | flops | bytes accessed | tf_op | source)
XLA Modules:
  0.0 116.8 jit_solution(12225551978958643934)
XLA Ops:
  0.0 0.7 add_and_fusion.1
  0.7 0.1 pad_add_fusion
  0.7 0.0 copy-start.1
  0.7 0.7 copy-done.1
  1.4 0.0 copy-start.3
  1.4 1.0 copy-done.3
  2.5 0.0 copy-start.5
  2.5 0.9 copy-done.5
  3.4 4.9 %spread.1 = (bf16[128,40,128]{2,1,0:T(8,128)(2,1)S(1)}, bf16[128,32,128]{2,1,0:T(8,128)(2,1)}) custom-call(f32[2,256,256]{2,1,0:T(8,128)S(1)} %copy-done.3, s32[1,256]{1,0:T(1,128)S(1)} %bitcast.6, s32[1,128]{1,0:T(1,128)S(1)} %pad_bitcast_fusion.info_ref, bf16[256,144]{1,0:T(8,128)(2,1)S(1)} %copy-done.5), custom_call_target="tpu_custom_call" | custom-call | flops 838860800 | bytes 3145728 | tf_op jit(solution)/shard_map/spread/pallas_call | solution.py:75
  8.2 31.5 %all_to_all.20.r_ref = bf16[128,40,128]{2,1,0:T(8,128)(2,1)S(1)} all-to-all(bf16[128,40,128]{2,1,0:T(8,128)(2,1)S(1)} %get-tuple-element.7), channel_id=1, replica_groups=mesh['tg'=2,'pw_0'=4,'pw_1'=4,'pw_2'=4] {'tg','pw_0','pw_1','pw_2'}, dimensions={0} | all-to-all | bytes 2621440 | tf_op jit(solution)/shard_map/all_to_all | solution.py:276
  39.8 0.0 copy-start
  39.8 0.0 copy-start.4
  39.8 0.0 copy-start.6
  39.8 0.0 copy-start.7
  39.8 0.0 copy-start.8
  39.8 5.9 %all-to-all-start.1 = ((bf16[128,32,128]{2,1,0:T(8,128)(2,1)}), bf16[128,32,128]{2,1,0:T(8,128)(2,1)S(1)}, u32[]{:S(2)}, u32[]{:S(2)}) async-start(bf16[128,32,128]{2,1,0:T(8,128)(2,1)} %get-tuple-element.8), calls=%async_computation.1 | async-start | bytes 2097152 | tf_op jit(solution)/shard_map/all_to_all | solution.py:276
  45.7 0.1 fusion
  45.8 0.1 slice_add_fusion
  45.9 0.1 reshape.19.cell_ref
  45.9 0.0 copy-done
  45.9 0.0 copy-done.4
  45.9 0.0 copy-done.6
  46.0 0.0 copy-done.7
  46.0 0.0 copy-done.8
  46.0 15.5 %plane.3 = bf16[128,32,128]{2,1,0:T(8,128)(2,1)} custom-call(s32[2048]{0:T(1024)S(1)} %reshape.19.cell_ref, bf16[128,40,128]{2,1,0:T(8,128)(2,1)S(1)} %all_to_all.20.r_ref, f32[128,128]{1,0:T(8,128)S(1)} %bitcast.8, bf16[256,144]{1,0:T(8,128)(2,1)S(1)} %copy-done.7, bf16[256,144]{1,0:T(8,128)(2,1)S(1)} %copy-done.6, bf16[144,256]{1,0:T(8,128)(2,1)S(1)} %copy-done, ...), custom_call_target="tpu_custom_call" | custom-call | flops 5046272000 | bytes 3145728 | tf_op jit(solution)/shard_map/plane/pallas_call | solution.py:200
  61.5 1.9 %all-to-all-done.1.r_ref = bf16[128,32,128]{2,1,0:T(8,128)(2,1)S(1)} async-done(((bf16[128,32,128]{2,1,0:T(8,128)(2,1)}), bf16[128,32,128]{2,1,0:T(8,128)(2,1)S(1)}, u32[]{:S(2)}, u32[]{:S(2)}) %all-to-all-start.1) | async-done | bytes 1048608 | tf_op jit(solution)/shard_map/all_to_all | solution.py:276
  63.4 7.9 %all-to-all-start.3 = ((bf16[128,32,128]{2,1,0:T(8,128)(2,1)}), bf16[128,32,128]{2,1,0:T(8,128)(2,1)S(1)}, u32[]{:S(2)}, u32[]{:S(2)}) async-start(bf16[128,32,128]{2,1,0:T(8,128)(2,1)} %plane.3), calls=%async_computation.3 | async-start | bytes 2097152 | tf_op jit(solution)/shard_map/all_to_all | solution.py:276
  71.3 15.5 %plane.2 = bf16[128,32,128]{2,1,0:T(8,128)(2,1)} custom-call(s32[2048]{0:T(1024)S(1)} %reshape.19.cell_ref, bf16[128,32,128]{2,1,0:T(8,128)(2,1)S(1)} %all-to-all-done.1.r_ref, f32[128,128]{1,0:T(8,128)S(1)} %bitcast.9, bf16[256,144]{1,0:T(8,128)(2,1)S(1)} %copy-done.7, bf16[256,144]{1,0:T(8,128)(2,1)S(1)} %copy-done.6, bf16[144,256]{1,0:T(8,128)(2,1)S(1)} %copy-done, ...), custom_call_target="tpu_custom_call" | custom-call | flops 5046272000 | bytes 3145728 | tf_op jit(solution)/shard_map/plane/pallas_call | solution.py:200
  86.8 0.0 copy-start.2
  86.8 2.2 %all-to-all-done.3.r_ref = bf16[128,32,128]{2,1,0:T(8,128)(2,1)S(1)} async-done(((bf16[128,32,128]{2,1,0:T(8,128)(2,1)}), bf16[128,32,128]{2,1,0:T(8,128)(2,1)S(1)}, u32[]{:S(2)}, u32[]{:S(2)}) %all-to-all-start.3) | async-done | bytes 1048608 | tf_op jit(solution)/shard_map/all_to_all | solution.py:276
  89.0 7.6 %all-to-all-start.2 = ((bf16[128,32,128]{2,1,0:T(8,128)(2,1)}), bf16[128,32,128]{2,1,0:T(8,128)(2,1)S(1)}, u32[]{:S(2)}, u32[]{:S(2)}) async-start(bf16[128,32,128]{2,1,0:T(8,128)(2,1)} %plane.2), calls=%async_computation.2 | async-start | bytes 2097152 | tf_op jit(solution)/shard_map/all_to_all | solution.py:276
  96.6 0.0 copy-done.2
  96.6 0.1 copy.11.place_ref
  96.7 2.5 %finish.2.rest_0_ = f32[2,256,256]{2,1,0:T(8,128)} custom-call(bf16[128,32,128]{2,1,0:T(8,128)(2,1)S(1)} %all-to-all-done.3.r_ref, s32[256,1]{1,0:T(8,128)S(1)} %copy.11.place_ref, bf16[144,256]{1,0:T(8,128)(2,1)S(1)} %copy-done), custom_call_target="tpu_custom_call" | custom-call | flops 318767104 | bytes 2097152 | tf_op jit(solution)/shard_map/finish/pallas_call | solution.py:256
  99.2 15.1 %all-to-all-done.2.r_ref = bf16[128,32,128]{2,1,0:T(8,128)(2,1)S(1)} async-done(((bf16[128,32,128]{2,1,0:T(8,128)(2,1)}), bf16[128,32,128]{2,1,0:T(8,128)(2,1)S(1)}, u32[]{:S(2)}, u32[]{:S(2)}) %all-to-all-start.2) | async-done | bytes 1048608 | tf_op jit(solution)/shard_map/all_to_all | solution.py:276
  114.3 2.5 %finish.3 = f32[2,256,256]{2,1,0:T(8,128)} custom-call(bf16[128,32,128]{2,1,0:T(8,128)(2,1)S(1)} %all-to-all-done.2.r_ref, s32[256,1]{1,0:T(8,128)S(1)} %copy.11.place_ref, bf16[144,256]{1,0:T(8,128)(2,1)S(1)} %copy-done, f32[2,256,256]{2,1,0:T(8,128)} %finish.2.rest_0_), custom_call_target="tpu_custom_call", output_to_operand_aliasing={{}: (3, {})} | custom-call | flops 318767104 | bytes 2097152 | tf_op jit(solution)/shard_map/finish/pallas_call | solution.py:256
  (1 shorter events, 0.0 us)
Async XLA Ops:
  0.7 0.7 copy-start.1
  1.4 1.0 copy-start.3
  2.5 0.9 copy-start.5
  39.8 6.2 %copy-start = (bf16[144,256]{1,0:T(8,128)(2,1)S(1)}, bf16[144,256]{1,0:T(8,128)(2,1)}, u32[]{:S(2)}) copy-start(bf16[144,256]{1,0:T(8,128)(2,1)} %constant.20.clone.ix_ref.i_ref) | copy-start | bytes 221188
  39.8 6.2 %copy-start.4 = (f32[128,128,1]{1,2,0:T(1,128)S(1)}, f32[128,128,1]{1,2,0:T(1,128)}, u32[]{:S(2)}) copy-start(f32[128,128,1]{1,2,0:T(1,128)} %param.11) | copy-start | bytes 196612
  39.8 6.2 %copy-start.6 = (bf16[256,144]{1,0:T(8,128)(2,1)S(1)}, bf16[256,144]{1,0:T(8,128)(2,1)}, u32[]{:S(2)}) copy-start(bf16[256,144]{1,0:T(8,128)(2,1)} %constant.19.clone.e_ref.ex_ref) | copy-start | bytes 221188
  39.8 6.2 %copy-start.7 = (bf16[256,144]{1,0:T(8,128)(2,1)S(1)}, bf16[256,144]{1,0:T(8,128)(2,1)}, u32[]{:S(2)}) copy-start(bf16[256,144]{1,0:T(8,128)(2,1)} %constant.18.clone.ey_ref) | copy-start | bytes 221188
  39.8 6.2 %copy-start.8 = (bf16[144,256]{1,0:T(8,128)(2,1)S(1)}, bf16[144,256]{1,0:T(8,128)(2,1)}, u32[]{:S(2)}) copy-start(bf16[144,256]{1,0:T(8,128)(2,1)} %constant.21.clone.iy_ref) | copy-start | bytes 221188
  39.8 23.6 %all-to-all-start.1 = ((bf16[128,32,128]{2,1,0:T(8,128)(2,1)}), bf16[128,32,128]{2,1,0:T(8,128)(2,1)S(1)}, u32[]{:S(2)}, u32[]{:S(2)}) async-start(bf16[128,32,128]{2,1,0:T(8,128)(2,1)} %get-tuple-element.8), calls=%async_computation.1 | async-start | bytes 2097152 | tf_op jit(solution)/shard_map/all_to_all | solution.py:276
  63.4 25.6 %all-to-all-start.3 = ((bf16[128,32,128]{2,1,0:T(8,128)(2,1)}), bf16[128,32,128]{2,1,0:T(8,128)(2,1)S(1)}, u32[]{:S(2)}, u32[]{:S(2)}) async-start(bf16[128,32,128]{2,1,0:T(8,128)(2,1)} %plane.3), calls=%async_computation.3 | async-start | bytes 2097152 | tf_op jit(solution)/shard_map/all_to_all | solution.py:276
  86.8 9.8 %copy-start.2 = (s32[256]{0:T(256)S(1)}, s32[256]{0:T(256)}, u32[]{:S(2)}) copy-start(s32[256]{0:T(256)} %param.9) | copy-start | bytes 3076
  89.0 25.3 %all-to-all-start.2 = ((bf16[128,32,128]{2,1,0:T(8,128)(2,1)}), bf16[128,32,128]{2,1,0:T(8,128)(2,1)S(1)}, u32[]{:S(2)}, u32[]{:S(2)}) async-start(bf16[128,32,128]{2,1,0:T(8,128)(2,1)} %plane.2), calls=%async_computation.2 | async-start | bytes 2097152 | tf_op jit(solution)/shard_map/all_to_all | solution.py:276
where the time goes:
time: 117 us
  Pallas kernels  40.9 us (35%)
  blocking collectives  31.5 us (27%)
  starting transfers between devices  21.4 us (18%)
  waiting for transfers between devices  19.1 us (16%)
  local copies, waits for them, and re-layouts  2.87 us (2%)
    all_to_all x1, blocking collectives, exchange(): return lax.all_to_all(value, TG_PW, split_axis=0, concat_axis=0, tiled=True)  31.5 us
    pallas_call x2, Pallas kernels, plane_pass(): pl.pallas_call(plane_kernel, out_shape=jax.ShapeDtypeStruct((owners, 2 *...  31.1 us
    all_to_all x3, starting transfers between devices, exchange(): return lax.all_to_all(value, TG_PW, split_axis=0, concat_axis=0, tiled=True)  21.4 us
    all_to_all x3, waiting for transfers between devices, exchange(): return lax.all_to_all(value, TG_PW, split_axis=0, concat_axis=0, tiled=True)  19.1 us
    pallas_call x2, Pallas kernels, finish(): pl.pallas_call(finish_kernel, grid=(1,), out_shape=jax.ShapeDtypeStruct((...  4.96 us
    pallas_call x1, Pallas kernels, spread(): pl.pallas_call(spread_kernel, out_shape=(jax.ShapeDtypeStruct((NR, 2 * SL...  4.87 us
    unnamed x18, local copies, waits for them, and re-layouts  2.65 us
  transfers between devices with their start and end apart: 3, of which 3 were waited for; matrix products, arithmetic and copies ran while one was open for 0% of the time, Pallas kernels for 29%

commit v1 on v0

--- a/solution.py
+++ b/solution.py
@@ -1,3 +1,5 @@
+import functools
+
 import numpy as np
 import jax
 import jax.numpy as jnp
@@ -13,10 +15,12 @@
 PAIRS = 33
 SLOT = 16
 LANES = 128
+PIECES = 4
 TG_PW = ("tg", "pw_0", "pw_1", "pw_2")
 BF = jnp.bfloat16
 F32 = jnp.float32
 VMEM = pl.BlockSpec(memory_space=pltpu.VMEM)
+HBM = pl.BlockSpec(memory_space=pltpu.HBM)
 SMEM = pl.BlockSpec(memory_space=pltpu.SMEM)
 
 
@@ -43,86 +47,139 @@
     return [jnp.asarray(t, BF) for t in (ahead_y, ahead_x, behind_x, behind_y)]
 
 
-def spread_kernel(c_ref, place_ref, info_ref, e_ref, a_ref, b_ref, t_ref):
+def spread_kernel(
+    half, c_hbm, place_hbm, column_ref, e_hbm, o_ref, c_ref, place_ref, e_ref, t_ref, sem
+):
+    first = pltpu.make_async_copy(place_hbm, place_ref, sem.at[2])
+    first.start()
+    copies = [
+        pltpu.make_async_copy(
+            c_hbm.at[p, :, pl.ds(half * LANES, LANES)], c_ref.at[p], sem.at[p]
+        )
+        for p in range(2)
+    ]
+    copies.append(pltpu.make_async_copy(e_hbm, e_ref, sem.at[3]))
+    for copy in copies:
+        copy.start()
+    first.wait()
     place = place_ref[...]
     row = (place >> 7) * BOX + ((place + HALF) & (NR - 1))
     at = lax.broadcasted_iota(jnp.int32, (SLOT * BOX, place.shape[1]), 0)
     select = jnp.where(at == row, 1.0, 0.0).astype(BF)
-    parts = [
-        jnp.dot(select, c_ref[p].astype(BF), preferred_element_type=F32) for p in range(2)
-    ]
+    for copy in copies:
+        copy.wait()
+    both = jnp.concatenate([c_ref[p].astype(BF) for p in range(2)], axis=1)
+    placed = jnp.dot(select, both, preferred_element_type=F32)
+    xs = []
     for s in range(SLOT):
-        x = jnp.concatenate([parts[p][s * BOX : (s + 1) * BOX] for p in range(2)], axis=0)
-        m = jnp.dot(e_ref[...], x.astype(BF), preferred_element_type=F32)
-        for h in range(2):
+        rows = placed[s * BOX : (s + 1) * BOX]
+        xs.append(jnp.concatenate([rows[:, :LANES], rows[:, LANES:]], axis=0).astype(BF))
+    for j in range(SLOT // 2):
+        x = jnp.concatenate(xs[2 * j : 2 * j + 2], axis=1)
+        m = jnp.dot(e_ref[...], x, preferred_element_type=F32)
+        for q in range(2):
             for p in range(2):
-                t_ref[h, pl.ds(2 * s + p, NR, stride=2 * SLOT), :] = m[
-                    p * NR : (p + 1) * NR, h * LANES : (h + 1) * LANES
+                t_ref[pl.ds(2 * (2 * j + q) + p, NR, stride=2 * SLOT), :] = m[
+                    p * NR : (p + 1) * NR, q * LANES : (q + 1) * LANES
                 ]
-    info = jnp.broadcast_to(info_ref[...], (8, LANES)).astype(F32).astype(BF)
-
-    @pl.loop(0, NR // 4)
-    def _(i):
-        for u in range(4):
-            k = i * 4 + u
+    if half == 0:
+        lane = lax.broadcasted_iota(jnp.int32, (8, LANES), 1)
+        info = jnp.zeros((8, LANES), jnp.int32)
+        for s in range(SLOT):
+            column = column_ref[s]
+            info = jnp.where(lane == s, ((column >> 7) + HALF) & (NR - 1), info)
+            info = jnp.where(lane == SLOT + s, (column + HALF) & (NR - 1), info)
+        info = info.astype(F32).astype(BF)
+
+    @pl.loop(0, NR // 8)
+    def _(i):
+        for u in range(8):
+            k = i * 8 + u
             rows = pl.ds(pl.multiple_of(k * 2 * SLOT, 2 * SLOT), 2 * SLOT)
-            a_ref[k, 0 : 2 * SLOT, :] = t_ref[0, rows, :].astype(BF)
-            a_ref[k, 2 * SLOT : 2 * SLOT + 8, :] = info
-            b_ref[k] = t_ref[1, rows, :].astype(BF)
-
-
-def spread(coeffs, place, info, ahead_z):
+            o_ref[k, 0 : 2 * SLOT, :] = t_ref[rows, :].astype(BF)
+            if half == 0:
+                o_ref[k, 2 * SLOT : 2 * SLOT + 8, :] = info
+
+
+def spread(half, coeffs, place, columns, ahead_z):
+    height = 2 * SLOT + (8 if half == 0 else 0)
     return pl.pallas_call(
-        spread_kernel,
-        out_shape=(
-            jax.ShapeDtypeStruct((NR, 2 * SLOT + 8, LANES), BF),
-            jax.ShapeDtypeStruct((NR, 2 * SLOT, LANES), BF),
-        ),
-        in_specs=[VMEM] * 4,
-        out_specs=(VMEM, VMEM),
-        scratch_shapes=[pltpu.VMEM((2, NR * 2 * SLOT, LANES), F32)],
-        compiler_params=pltpu.CompilerParams(vmem_limit_bytes=40 << 20),
+        functools.partial(spread_kernel, half),
+        out_shape=jax.ShapeDtypeStruct((NR, height, LANES), BF),
+        in_specs=[HBM, HBM, SMEM, HBM],
+        out_specs=VMEM,
+        scratch_shapes=[
+            pltpu.VMEM((2, place.shape[1], LANES), F32),
+            pltpu.VMEM(place.shape, jnp.int32),
+            pltpu.VMEM(ahead_z.shape, BF),
+            pltpu.VMEM((NR * 2 * SLOT, LANES), F32),
+            pltpu.SemaphoreType.DMA((4,)),
+        ],
+        compiler_params=pltpu.CompilerParams(vmem_limit_bytes=62 << 20),
         cost_estimate=pl.CostEstimate(
-            flops=2 * (1152 * 256 * 512 + 4096 * 256 * 256), bytes_accessed=3 << 20, transcendentals=0
+            flops=2 * (1152 + 2048) * 256 * 256, bytes_accessed=2 << 20, transcendentals=0
         ),
         name="spread",
-    )(coeffs, place, info, ahead_z)
+    )(coeffs, place, columns, ahead_z)
 
 
 def plane_kernel(
-    cell_ref, r_ref, v_ref, ey_ref, ex_ref, ix_ref, iy_ref, o_ref, f_ref, g_ref, s_ref, w_ref
+    cell_ref, r_hbm, v_hbm, ey_hbm, ex_hbm, ix_hbm, iy_hbm, o_hbm,
+    r_ref, v_ref, ey_ref, ex_ref, ix_ref, iy_ref, f_ref, g_ref, s_ref, w_ref, sem,
 ):
     sticks = f_ref.shape[0] // 2
     owners = r_ref.shape[0]
     per = 2 * SLOT
     two = 2 * BOX
+    share = owners // PIECES
+    pieces = [
+        pltpu.make_async_copy(
+            r_hbm.at[pl.ds(q * share, share), pl.ds(0, per), :],
+            r_ref.at[pl.ds(q * share, share)],
+            sem.at[q],
+        )
+        for q in range(PIECES)
+    ]
+    fixed = [
+        pltpu.make_async_copy(src, dst, sem.at[PIECES + n])
+        for n, (src, dst) in enumerate(
+            [(ey_hbm, ey_ref), (v_hbm, v_ref), (ex_hbm, ex_ref), (ix_hbm, ix_ref), (iy_hbm, iy_ref)]
+        )
+    ]
+    for copy in pieces + fixed:
+        copy.start()
     blank = jnp.zeros((two, LANES), F32)
 
-    @pl.loop(0, 2 * PAIRS)
+    @pl.loop(0, PAIRS)
     def _(x):
-        g_ref[pl.ds(pl.multiple_of(x * two, 8), two), :] = blank
-
-    @pl.loop(0, NR // 8)
-    def _(i):
-        for u in range(16):
-            s_ref[pl.ds(pl.multiple_of((i * 16 + u) * BOX + 64, 8), 8), :] = blank[:8]
-
-    @pl.loop(0, owners // 8)
-    def _(i):
-        for u in range(8):
-            o = i * 8 + u
-            f_ref[pl.ds(pl.multiple_of(o * per, per), per), :] = r_ref[o, 0:per, :].astype(F32)
+        g_ref[pl.ds(pl.multiple_of(x * 2 * two, 8), two), :] = blank
+        g_ref[pl.ds(pl.multiple_of(x * 2 * two + two, 8), two), :] = blank
+
+    @pl.loop(0, NR // 16)
+    def _(i):
+        for u in range(32):
+            s_ref[pl.ds(pl.multiple_of((i * 32 + u) * BOX + 64, 8), 8), :] = blank[:8]
 
     step = 32
-
-    @pl.loop(0, sticks // step)
-    def _(i):
-        for u in range(step):
-            c = cell_ref[i * step + u]
-            g_ref[pl.ds(2 * c, 2), :] = f_ref[
-                pl.ds(pl.multiple_of(i * 2 * step, 2 * step) + 2 * u, 2), :
-            ]
-
+    for q in range(PIECES):
+        pieces[q].wait()
+
+        @pl.loop(q * share // 8, (q + 1) * share // 8)
+        def _(i):
+            for u in range(8):
+                o = i * 8 + u
+                f_ref[pl.ds(pl.multiple_of(o * per, per), per), :] = r_ref[o].astype(F32)
+
+        @pl.loop(q * sticks // PIECES // step, (q + 1) * sticks // PIECES // step)
+        def _(i):
+            for u in range(step):
+                c = cell_ref[i * step + u]
+                g_ref[pl.ds(2 * c, 2), :] = f_ref[
+                    pl.ds(pl.multiple_of(i * 2 * step, 2 * step) + 2 * u, 2), :
+                ]
+
+    for copy in fixed:
+        copy.wait()
     turn = 11
 
     @pl.loop(0, PAIRS // turn)
@@ -180,19 +237,28 @@
             g_ref[pl.ds(pl.multiple_of(r0, 8), two), :] = m[:, :LANES]
             g_ref[pl.ds(pl.multiple_of(r0 + two, 8), two), :] = m[:, LANES:]
 
-    @pl.loop(0, sticks // step)
-    def _(i):
-        for u in range(step):
-            c = cell_ref[i * step + u]
-            f_ref[pl.ds(pl.multiple_of(i * 2 * step, 2 * step) + 2 * u, 2), :] = g_ref[
-                pl.ds(2 * c, 2), :
-            ]
-
-    @pl.loop(0, owners // 8)
-    def _(i):
-        for u in range(8):
-            o = i * 8 + u
-            o_ref[o] = f_ref[pl.ds(pl.multiple_of(o * per, per), per), :].astype(BF)
+    backs = []
+    for q in range(PIECES):
+
+        @pl.loop(q * sticks // PIECES // step, (q + 1) * sticks // PIECES // step)
+        def _(i):
+            for u in range(step):
+                c = cell_ref[i * step + u]
+                f_ref[pl.ds(pl.multiple_of(i * 2 * step, 2 * step) + 2 * u, 2), :] = g_ref[
+                    pl.ds(2 * c, 2), :
+                ]
+
+        @pl.loop(q * share // 8, (q + 1) * share // 8)
+        def _(i):
+            for u in range(8):
+                o = i * 8 + u
+                r_ref[o] = f_ref[pl.ds(pl.multiple_of(o * per, per), per), :].astype(BF)
+
+        part = pl.ds(q * share, share)
+        backs.append(pltpu.make_async_copy(r_ref.at[part], o_hbm.at[part], sem.at[q]))
+        backs[q].start()
+    for copy in backs:
+        copy.wait()
 
 
 def plane_pass(cells, received, volume, tabs):
@@ -200,15 +266,19 @@
     return pl.pallas_call(
         plane_kernel,
         out_shape=jax.ShapeDtypeStruct((owners, 2 * SLOT, LANES), BF),
-        in_specs=[SMEM] + [VMEM] * 6,
-        out_specs=VMEM,
+        in_specs=[SMEM] + [HBM] * 6,
+        out_specs=HBM,
         scratch_shapes=[
+            pltpu.VMEM((owners, 2 * SLOT, LANES), BF),
+            pltpu.VMEM(volume.shape, F32),
+            *[pltpu.VMEM(t.shape, BF) for t in tabs],
             pltpu.VMEM((owners * 2 * SLOT, LANES), F32),
             pltpu.VMEM((2 * PAIRS * 2 * BOX, LANES), F32),
             pltpu.VMEM((2 * NR * BOX, LANES), F32),
             pltpu.VMEM((16, 2 * NR, 2 * LANES), BF),
+            pltpu.SemaphoreType.DMA((PIECES + 5,)),
         ],
-        compiler_params=pltpu.CompilerParams(vmem_limit_bytes=40 << 20),
+        compiler_params=pltpu.CompilerParams(vmem_limit_bytes=62 << 20),
         cost_estimate=pl.CostEstimate(
             flops=2 * 38500 * 256 * 256, bytes_accessed=3 << 20, transcendentals=0
         ),
@@ -216,9 +286,13 @@
     )(cells, received, volume, *tabs)
 
 
-def finish_kernel(r_ref, place_ref, i_ref, *rest):
-    o_ref, t_ref, sp_ref = rest[-3:]
+def finish_kernel(half, r_ref, place_ref, i_ref, *rest):
+    o_hbm, t_ref, sp_ref, out_ref, sem = rest[-5:]
     per = 2 * SLOT
+    place = place_ref[...]
+    row = (place >> 7) * BOX + ((place + HALF) & (NR - 1))
+    at = lax.broadcasted_iota(jnp.int32, (place.shape[0], SLOT * BOX), 1)
+    select = jnp.where(at == row, 1.0 / NR**3, 0.0).astype(BF)
 
     @pl.loop(0, NR // 8)
     def _(i):
@@ -241,27 +315,33 @@
                 sp_ref[rows, p * LANES : (p + 1) * LANES] = m[
                     p * BOX : (p + 1) * BOX, q * LANES : (q + 1) * LANES
                 ]
-    place = place_ref[...]
-    row = (place >> 7) * BOX + ((place + HALF) & (NR - 1))
-    at = lax.broadcasted_iota(jnp.int32, (place.shape[0], SLOT * BOX), 1)
-    select = jnp.where(at == row, 1.0 / NR**3, 0.0).astype(BF)
     out = jnp.dot(select, sp_ref[...].astype(BF), preferred_element_type=F32)
+    sends = []
     for p in range(2):
-        o_ref[p] = out[:, p * LANES : (p + 1) * LANES]
+        out_ref[p] = out[:, p * LANES : (p + 1) * LANES]
+        sends.append(
+            pltpu.make_async_copy(
+                out_ref.at[p], o_hbm.at[p, :, pl.ds(half * LANES, LANES)], sem.at[p]
+            )
+        )
+        sends[p].start()
+    for copy in sends:
+        copy.wait()
 
 
 def finish(returned, place, behind_z, half, into=None):
     count = place.shape[0]
     extra = [] if into is None else [into]
     return pl.pallas_call(
-        finish_kernel,
-        grid=(1,),
+        functools.partial(finish_kernel, half),
         out_shape=jax.ShapeDtypeStruct((2, count, 2 * LANES), F32),
-        in_specs=[VMEM] * 3 + [pl.BlockSpec(memory_space=pl.ANY)] * len(extra),
-        out_specs=pl.BlockSpec((2, count, LANES), lambda i: (0, 0, half)),
+        in_specs=[VMEM] * 3 + [HBM] * len(extra),
+        out_specs=HBM,
         scratch_shapes=[
             pltpu.VMEM((NR * 2 * SLOT, LANES), F32),
             pltpu.VMEM((SLOT * BOX, 2 * LANES), F32),
+            pltpu.VMEM((2, count, LANES), F32),
+            pltpu.SemaphoreType.DMA((2,)),
         ],
         input_output_aliases={} if into is None else {3: 0},
         compiler_params=pltpu.CompilerParams(vmem_limit_bytes=24 << 20),
@@ -279,15 +359,14 @@
 def body(coeffs, g_place, stick_column, potential):
     tabs = tables()
     ahead_z, behind_z = tabs[1], tabs[2]
-    x_box = ((stick_column >> 7) + HALF) & (NR - 1)
-    y_box = (stick_column + HALF) & (NR - 1)
-    info = jnp.pad(jnp.concatenate([x_box, y_box]), (0, LANES - 2 * SLOT)).reshape(1, LANES)
-    sent_a, sent_b = spread(coeffs, g_place.reshape(1, -1), info, ahead_z)
+    row = g_place.reshape(1, -1)
+    sent_a = spread(0, coeffs, row, stick_column, ahead_z)
+    sent_b = spread(1, coeffs, row, stick_column, ahead_z)
     got_a = exchange(sent_a)
     got_b = exchange(sent_b)
+    volume = potential.reshape(NR, NR)
     column = got_a[:, 2 * SLOT, : 2 * SLOT].astype(F32).astype(jnp.int32)
     cells = (column[:, :SLOT] * BOX + column[:, SLOT:]).reshape(-1)
-    volume = potential.reshape(NR, NR)
     done_a = plane_pass(cells, got_a, volume, tabs)
     back_a = exchange(done_a)
     done_b = plane_pass(cells, got_b, volume, tabs)

time: 117 us -> 116 us (level)
  blocking collectives: 31.5 us -> 0 us
  waiting for transfers between devices: 19.1 us -> 33 us
  starting transfers between devices: 21.4 us -> 34.9 us
  Pallas kernels: 40.9 us -> 46.3 us
  local copies, waits for them, and re-layouts: 2.87 us -> 0.83 us
    all_to_all x1 -> x0, blocking collectives: 31.5 us -> none  [exchange(): return lax.all_to_all(value, TG_PW, split_axis=0, concat_axis=0, tiled=True)]
    all_to_all x3 -> x4, waiting for transfers between devices: 19.1 us -> 33 us  [exchange(): return lax.all_to_all(value, TG_PW, split_axis=0, concat_axis=0, tiled=True)]
    all_to_all x3 -> x4, starting transfers between devices: 21.4 us -> 34.9 us  [exchange(): return lax.all_to_all(value, TG_PW, split_axis=0, concat_axis=0, tiled=True)]
    pallas_call x3 -> x4, Pallas kernels: 9.83 us -> 14.6 us  [the longest x2 9.39 us: spread(): pl.pallas_call(functools.partial(spread_kernel, half), out_shape=jax.Shap...]
    unnamed x18 -> x6, local copies, waits for them, and re-layouts: 2.65 us -> 0.02 us
  transfers between devices with their start and end apart: 3 -> 4, of which waited for: 3 -> 4; matrix products, arithmetic and copies ran while one was open for 0% -> 1% of each run, Pallas kernels for 29% -> 34%
where the time goes in v1:
time: 116 us
  Pallas kernels  46.3 us (40%)
  starting transfers between devices  34.9 us (30%)
  waiting for transfers between devices  33 us (28%)
    all_to_all x4, starting transfers between devices, exchange(): return lax.all_to_all(value, TG_PW, split_axis=0, concat_axis=0, tiled=True)  34.9 us
    all_to_all x4, waiting for transfers between devices, exchange(): return lax.all_to_all(value, TG_PW, split_axis=0, concat_axis=0, tiled=True)  33 us
    pallas_call x2, Pallas kernels, plane_pass(): pl.pallas_call(plane_kernel, out_shape=jax.ShapeDtypeStruct((owners, 2 *...  31.7 us
    pallas_call x2, Pallas kernels, spread(): pl.pallas_call(functools.partial(spread_kernel, half), out_shape=jax.Shap...  9.39 us
    pallas_call x2, Pallas kernels, finish(): pl.pallas_call(functools.partial(finish_kernel, half), out_shape=jax.Shap...  5.25 us
  transfers between devices with their start and end apart: 4, of which 4 were waited for; matrix products, arithmetic and copies ran while one was open for 1% of the time, Pallas kernels for 34%

profile of v1, /device:TPU:1, one launch (start us, length us, event | category | flops | bytes accessed | tf_op | source)
XLA Modules:
  0.0 115.5 jit_solution(14029033885365280897)
XLA Ops:
  0.0 4.8 %spread.2 = bf16[128,40,128]{2,1,0:T(8,128)(2,1)} custom-call(f32[2,256,256]{2,1,0:T(8,128)} %c_hbm.3, s32[1,256]{1,0:T(1,128)} %bitcast.5, s32[16]{0:T(128)} %column_ref.3, bf16[256,144]{1,0:T(8,128)(2,1)} %constant.11.clone.e_hbm.ex_hbm), custom_call_target="tpu_custom_call" | custom-call | flops 419430400 | bytes 2097152 | tf_op jit(solution)/shard_map/spread/pallas_call | solution.py:106
  4.8 11.5 %all-to-all-start = ((bf16[128,40,128]{2,1,0:T(8,128)(2,1)}), bf16[128,40,128]{2,1,0:T(8,128)(2,1)S(1)}, u32[]{:S(2)}, u32[]{:S(2)}) async-start(bf16[128,40,128]{2,1,0:T(8,128)(2,1)} %spread.2), calls=%async_computation | async-start | bytes 2621440 | tf_op jit(solution)/shard_map/all_to_all | solution.py:356
  16.3 4.6 %spread.3 = bf16[128,32,128]{2,1,0:T(8,128)(2,1)} custom-call(f32[2,256,256]{2,1,0:T(8,128)} %c_hbm.3, s32[1,256]{1,0:T(1,128)} %bitcast.6, s32[16]{0:T(128)} %column_ref.3, bf16[256,144]{1,0:T(8,128)(2,1)} %constant.11.clone.e_hbm.ex_hbm), custom_call_target="tpu_custom_call" | custom-call | flops 419430400 | bytes 2097152 | tf_op jit(solution)/shard_map/spread/pallas_call | solution.py:106
  20.9 15.6 %all-to-all-done.r_hbm = bf16[128,40,128]{2,1,0:T(8,128)(2,1)S(1)} async-done(((bf16[128,40,128]{2,1,0:T(8,128)(2,1)}), bf16[128,40,128]{2,1,0:T(8,128)(2,1)S(1)}, u32[]{:S(2)}, u32[]{:S(2)}) %all-to-all-start) | async-done | bytes 1310752 | tf_op jit(solution)/shard_map/all_to_all | solution.py:356
  36.5 0.0 copy-start.1
  36.5 6.4 %all-to-all-start.1 = ((bf16[128,32,128]{2,1,0:T(8,128)(2,1)}), bf16[128,32,128]{2,1,0:T(8,128)(2,1)}, u32[]{:S(2)}, u32[]{:S(2)}) async-start(bf16[128,32,128]{2,1,0:T(8,128)(2,1)} %spread.3), calls=%async_computation.1 | async-start | bytes 2097152 | tf_op jit(solution)/shard_map/all_to_all | solution.py:356
  42.9 0.1 fusion
  42.9 0.1 slice_add_fusion
  43.0 0.7 reshape.15.cell_ref
  43.7 0.0 copy-done.1
  43.7 15.8 %plane.3 = bf16[128,32,128]{2,1,0:T(8,128)(2,1)} custom-call(s32[2048]{0:T(1024)} %reshape.15.cell_ref, bf16[128,40,128]{2,1,0:T(8,128)(2,1)} %copy-done.1, f32[128,128]{1,0:T(8,128)} %bitcast.8, bf16[256,144]{1,0:T(8,128)(2,1)} %constant.10.clone.ey_hbm, bf16[256,144]{1,0:T(8,128)(2,1)} %constant.11.clone.e_hbm.ex_hbm, ...), custom_call_target="tpu_custom_call" | custom-call | flops 5046272000 | bytes 3145728 | tf_op jit(solution)/shard_map/plane/pallas_call | solution.py:266
  59.6 0.7 all-to-all-done.1.r_hbm
  60.2 9.1 %all-to-all-start.3 = ((bf16[128,32,128]{2,1,0:T(8,128)(2,1)}), bf16[128,32,128]{2,1,0:T(8,128)(2,1)S(1)}, u32[]{:S(2)}, u32[]{:S(2)}) async-start(bf16[128,32,128]{2,1,0:T(8,128)(2,1)} %plane.3), calls=%async_computation.3 | async-start | bytes 2097152 | tf_op jit(solution)/shard_map/all_to_all | solution.py:356
  69.3 15.9 %plane.2 = bf16[128,32,128]{2,1,0:T(8,128)(2,1)} custom-call(s32[2048]{0:T(1024)} %reshape.15.cell_ref, bf16[128,32,128]{2,1,0:T(8,128)(2,1)} %all-to-all-done.1.r_hbm, f32[128,128]{1,0:T(8,128)} %bitcast.9, bf16[256,144]{1,0:T(8,128)(2,1)} %constant.10.clone.ey_hbm, bf16[256,144]{1,0:T(8,128)(2,1)} %constant.11.clone.e_hbm.ex_hbm, ...), custom_call_target="tpu_custom_call" | custom-call | flops 5046272000 | bytes 3145728 | tf_op jit(solution)/shard_map/plane/pallas_call | solution.py:266
  85.2 0.0 copy-start.2
  85.2 0.0 copy-start
  85.2 1.8 %all-to-all-done.3.r_ref = bf16[128,32,128]{2,1,0:T(8,128)(2,1)S(1)} async-done(((bf16[128,32,128]{2,1,0:T(8,128)(2,1)}), bf16[128,32,128]{2,1,0:T(8,128)(2,1)S(1)}, u32[]{:S(2)}, u32[]{:S(2)}) %all-to-all-start.3) | async-done | bytes 1048608 | tf_op jit(solution)/shard_map/all_to_all | solution.py:356
  87.1 8.0 %all-to-all-start.2 = ((bf16[128,32,128]{2,1,0:T(8,128)(2,1)}), bf16[128,32,128]{2,1,0:T(8,128)(2,1)S(1)}, u32[]{:S(2)}, u32[]{:S(2)}) async-start(bf16[128,32,128]{2,1,0:T(8,128)(2,1)} %plane.2), calls=%async_computation.2 | async-start | bytes 2097152 | tf_op jit(solution)/shard_map/all_to_all | solution.py:356
  95.0 0.0 copy-done.2
  95.0 0.1 copy.11.place_ref
  95.2 0.0 copy-done
  95.2 2.6 %finish.2.rest_0_ = f32[2,256,256]{2,1,0:T(8,128)} custom-call(bf16[128,32,128]{2,1,0:T(8,128)(2,1)S(1)} %all-to-all-done.3.r_ref, s32[256,1]{1,0:T(8,128)S(1)} %copy.11.place_ref, bf16[144,256]{1,0:T(8,128)(2,1)S(1)} %copy-done), custom_call_target="tpu_custom_call" | custom-call | flops 318767104 | bytes 2097152 | tf_op jit(solution)/shard_map/finish/pallas_call | solution.py:335
  97.8 14.9 %all-to-all-done.2.r_ref = bf16[128,32,128]{2,1,0:T(8,128)(2,1)S(1)} async-done(((bf16[128,32,128]{2,1,0:T(8,128)(2,1)}), bf16[128,32,128]{2,1,0:T(8,128)(2,1)S(1)}, u32[]{:S(2)}, u32[]{:S(2)}) %all-to-all-start.2) | async-done | bytes 1048608 | tf_op jit(solution)/shard_map/all_to_all | solution.py:356
  112.7 2.6 %finish.3 = f32[2,256,256]{2,1,0:T(8,128)} custom-call(bf16[128,32,128]{2,1,0:T(8,128)(2,1)S(1)} %all-to-all-done.2.r_ref, s32[256,1]{1,0:T(8,128)S(1)} %copy.11.place_ref, bf16[144,256]{1,0:T(8,128)(2,1)S(1)} %copy-done, f32[2,256,256]{2,1,0:T(8,128)} %finish.2.rest_0_), custom_call_target="tpu_custom_call", output_to_operand_aliasing={{}: (3, {})} | custom-call | flops 318767104 | bytes 2097152 | tf_op jit(solution)/shard_map/finish/pallas_call | solution.py:335
Async XLA Ops:
  4.8 31.7 %all-to-all-start = ((bf16[128,40,128]{2,1,0:T(8,128)(2,1)}), bf16[128,40,128]{2,1,0:T(8,128)(2,1)S(1)}, u32[]{:S(2)}, u32[]{:S(2)}) async-start(bf16[128,40,128]{2,1,0:T(8,128)(2,1)} %spread.2), calls=%async_computation | async-start | bytes 2621440 | tf_op jit(solution)/shard_map/all_to_all | solution.py:356
  36.5 7.2 %copy-start.1 = (bf16[128,40,128]{2,1,0:T(8,128)(2,1)}, bf16[128,40,128]{2,1,0:T(8,128)(2,1)S(1)}, u32[]{:S(2)}) copy-start(bf16[128,40,128]{2,1,0:T(8,128)(2,1)S(1)} %all-to-all-done.r_hbm) | copy-start | bytes 3932164
  36.5 23.7 %all-to-all-start.1 = ((bf16[128,32,128]{2,1,0:T(8,128)(2,1)}), bf16[128,32,128]{2,1,0:T(8,128)(2,1)}, u32[]{:S(2)}, u32[]{:S(2)}) async-start(bf16[128,32,128]{2,1,0:T(8,128)(2,1)} %spread.3), calls=%async_computation.1 | async-start | bytes 2097152 | tf_op jit(solution)/shard_map/all_to_all | solution.py:356
  60.2 26.8 %all-to-all-start.3 = ((bf16[128,32,128]{2,1,0:T(8,128)(2,1)}), bf16[128,32,128]{2,1,0:T(8,128)(2,1)S(1)}, u32[]{:S(2)}, u32[]{:S(2)}) async-start(bf16[128,32,128]{2,1,0:T(8,128)(2,1)} %plane.3), calls=%async_computation.3 | async-start | bytes 2097152 | tf_op jit(solution)/shard_map/all_to_all | solution.py:356
  85.2 9.8 %copy-start.2 = (s32[256]{0:T(256)S(1)}, s32[256]{0:T(256)}, u32[]{:S(2)}) copy-start(s32[256]{0:T(256)} %param.9) | copy-start | bytes 3076
  85.2 10.0 %copy-start = (bf16[144,256]{1,0:T(8,128)(2,1)S(1)}, bf16[144,256]{1,0:T(8,128)(2,1)}, u32[]{:S(2)}) copy-start(bf16[144,256]{1,0:T(8,128)(2,1)} %constant.12.clone.ix_hbm.i_ref) | copy-start | bytes 221188
  87.1 25.7 %all-to-all-start.2 = ((bf16[128,32,128]{2,1,0:T(8,128)(2,1)}), bf16[128,32,128]{2,1,0:T(8,128)(2,1)S(1)}, u32[]{:S(2)}, u32[]{:S(2)}) async-start(bf16[128,32,128]{2,1,0:T(8,128)(2,1)} %plane.2), calls=%async_computation.2 | async-start | bytes 2097152 | tf_op jit(solution)/shard_map/all_to_all | solution.py:356

commit v2 on v1

v2 whole, which is shorter than its diff:
```python
import functools

import numpy as np
import jax
import jax.numpy as jnp
from jax import lax
from jax.experimental import pallas as pl
from jax.experimental.pallas import tpu as pltpu
from jax.sharding import Mesh
from jax.sharding import PartitionSpec as P

NR = 128
HALF = 32
BOX = 72
SIDE = 65
SLOT = 16
LANES = 128
PER = 4 * SLOT
PIECES = 4
TG_PW = ("tg", "pw_0", "pw_1", "pw_2")
BF = jnp.bfloat16
F32 = jnp.float32
VMEM = pl.BlockSpec(memory_space=pltpu.VMEM)
HBM = pl.BlockSpec(memory_space=pltpu.HBM)
SMEM = pl.BlockSpec(memory_space=pltpu.SMEM)


def complex_table(rows, cols, sign, keep_rows, keep_cols):
    angle = 2.0 * np.pi / NR * (np.outer(rows, cols) % NR)
    keep = keep_rows[:, None] * keep_cols[None, :]
    c = np.cos(angle) * keep
    s = sign * np.sin(angle) * keep
    return np.stack([np.stack([c, -s], 1), np.stack([s, c], 1)]).astype(np.float32)


def tables():
    full = np.arange(NR)
    box = np.arange(BOX) - HALF
    keep_box = (np.arange(BOX) <= 2 * HALF).astype(np.float32)
    keep_all = np.ones(NR, np.float32)
    ahead = complex_table(full, box, 1.0, keep_all, keep_box)
    behind = complex_table(box, full, -1.0, keep_box, keep_all)
    wide, tall = 2 * NR, 2 * BOX
    ahead_x = ahead.reshape(wide, tall)
    behind_x = behind.reshape(tall, wide)
    behind_y = behind.transpose(0, 1, 3, 2).reshape(tall, wide)
    ahead_y = ahead.transpose(1, 0, 2, 3).reshape(wide, tall)
    return [jnp.asarray(t, BF) for t in (ahead_x, behind_x, behind_y, ahead_y)]


def spread_kernel(
    c_hbm, place_hbm, column_ref, e_hbm, o_hbm, c_ref, place_ref, e_ref, t_ref, o_ref, sem
):
    first = pltpu.make_async_copy(place_hbm, place_ref, sem.at[PIECES])
    first.start()
    copies = [pltpu.make_async_copy(c_hbm.at[p], c_ref.at[p], sem.at[p]) for p in range(2)]
    copies.append(pltpu.make_async_copy(e_hbm, e_ref, sem.at[2]))
    for copy in copies:
        copy.start()
    first.wait()
    place = place_ref[...]
    row = (place >> 7) * BOX + ((place + HALF) & (NR - 1))
    at = lax.broadcasted_iota(jnp.int32, (SLOT * BOX, place.shape[1]), 0)
    select = jnp.where(at == row, 1.0, 0.0).astype(BF)
    lane = lax.broadcasted_iota(jnp.int32, (8, LANES), 1)
    info = jnp.zeros((8, LANES), jnp.int32)
    for s in range(SLOT):
        column = column_ref[s]
        info = jnp.where(lane == s, ((column >> 7) + HALF) & (NR - 1), info)
        info = jnp.where(lane == SLOT + s, (column + HALF) & (NR - 1), info)
    info = info.astype(F32).astype(BF)
    for copy in copies:
        copy.wait()
    both = jnp.concatenate([c_ref[p].astype(BF) for p in range(2)], axis=1)
    placed = jnp.dot(select, both, preferred_element_type=F32)
    xs = []
    for s in range(SLOT):
        rows = placed[s * BOX : (s + 1) * BOX]
        xs.append(
            jnp.concatenate([rows[:, : 2 * LANES], rows[:, 2 * LANES :]], axis=0).astype(BF)
        )
    for s in range(SLOT):
        m = jnp.dot(e_ref[...], xs[s], preferred_element_type=F32)
        for h in range(2):
            for p in range(2):
                t_ref[pl.ds(4 * s + 2 * h + p, NR, stride=PER), :] = m[
                    p * NR : (p + 1) * NR, h * LANES : (h + 1) * LANES
                ]
    share = NR // PIECES
    sends = []
    for q in range(PIECES):

        @pl.loop(q * share // 4, (q + 1) * share // 4)
        def _(i):
            for u in range(4):
                k = i * 4 + u
                rows = pl.ds(pl.multiple_of(k * PER, PER), PER)
                o_ref[k, 0:PER, :] = t_ref[rows, :].astype(BF)
                o_ref[k, PER : PER + 8, :] = info

        part = pl.ds(q * share, share)
        sends.append(pltpu.make_async_copy(o_ref.at[part], o_hbm.at[part], sem.at[q]))
        sends[q].start()
    for copy in sends:
        copy.wait()


def spread(coeffs, place, columns, ahead_z):
    out = jax.ShapeDtypeStruct((NR, PER + 8, LANES), BF)
    return pl.pallas_call(
        spread_kernel,
        out_shape=out,
        in_specs=[HBM, HBM, SMEM, HBM],
        out_specs=HBM,
        scratch_shapes=[
            pltpu.VMEM(coeffs.shape, F32),
            pltpu.VMEM(place.shape, jnp.int32),
            pltpu.VMEM(ahead_z.shape, BF),
            pltpu.VMEM((NR * PER, LANES), F32),
            pltpu.VMEM(out.shape, BF),
            pltpu.SemaphoreType.DMA((PIECES + 1,)),
        ],
        compiler_params=pltpu.CompilerParams(vmem_limit_bytes=62 << 20),
        cost_estimate=pl.CostEstimate(
            flops=2 * (2304 + 4096) * 256 * 256, bytes_accessed=3 << 20, transcendentals=0
        ),
        name="spread",
    )(coeffs, place, columns, ahead_z)


def plane_kernel(
    cell_ref, r_in, v_hbm, ey_hbm, ex_hbm, ix_hbm, iy_hbm, o_ref,
    v_ref, ey_ref, ex_ref, ix_ref, iy_ref, f_ref, g_ref, s_ref, w_ref, sem,
):
    owners = o_ref.shape[0]
    sticks = owners * SLOT
    tall = 2 * BOX
    share = owners // PIECES
    fixed = [
        pltpu.make_async_copy(src, dst, sem.at[n])
        for n, (src, dst) in enumerate(
            [(ey_hbm, ey_ref), (v_hbm, v_ref), (ex_hbm, ex_ref), (ix_hbm, ix_ref), (iy_hbm, iy_ref)]
        )
    ]
    for copy in fixed:
        copy.start()
    blank = jnp.zeros((4 * BOX, LANES), F32)

    @pl.loop(0, SIDE)
    def _(x):
        g_ref[pl.ds(pl.multiple_of(x * 4 * BOX, 8), 4 * BOX), :] = blank

    @pl.loop(0, NR // 8)
    def _(i):
        for u in range(16):
            for h in range(2):
                s_ref[h, pl.ds(pl.multiple_of((i * 16 + u) * BOX + 64, 8), 8), :] = blank[:8]

    step = 32
    for q in range(PIECES):

        @pl.loop(q * share // 4, (q + 1) * share // 4)
        def _(i):
            for u in range(4):
                o = i * 4 + u
                f_ref[pl.ds(pl.multiple_of(o * PER, PER), PER), :] = r_in[
                    o, 0:PER, :
                ].astype(F32)

        @pl.loop(q * sticks // PIECES // step, (q + 1) * sticks // PIECES // step)
        def _(i):
            for u in range(step):
                c = cell_ref[i * step + u]
                g_ref[pl.ds(pl.multiple_of(4 * c, 4), 4), :] = f_ref[
                    pl.ds(pl.multiple_of(i * 4 * step, 4 * step) + 4 * u, 4), :
                ]

    for copy in fixed:
        copy.wait()
    turn = 13

    @pl.loop(0, SIDE // turn)
    def _(i):
        xs = []
        for u in range(turn):
            r0 = (i * turn + u) * 4 * BOX
            halves = [
                jnp.concatenate(
                    [g_ref[pl.ds(r0 + 2 * h + p, BOX, stride=4), :] for p in range(2)], axis=0
                )
                for h in range(2)
            ]
            xs.append(jnp.concatenate(halves, axis=1).astype(BF))
        for u in range(turn):
            m = jnp.dot(ey_ref[...], xs[u], preferred_element_type=F32)
            for h in range(2):
                s_ref[h, pl.ds(i * turn + u, 2 * NR, stride=BOX), :] = m[
                    :, h * LANES : (h + 1) * LANES
                ]

    lane = lax.broadcasted_iota(jnp.int32, (NR, NR), 1)
    v = v_ref[...]
    batch = 16

    @pl.loop(0, NR // batch)
    def _(i):
        xs = []
        for u in range(batch):
            rows = pl.ds(pl.multiple_of((i * batch + u) * tall, 8), tall)
            xs.append(jnp.concatenate([s_ref[h, rows, :].astype(BF) for h in range(2)], axis=1))
        for u in range(batch):
            psi = jnp.dot(ex_ref[...], xs[u], preferred_element_type=F32)
            column = jnp.sum(
                jnp.where(lane == i * batch + u, v, 0.0), axis=1, keepdims=True
            )
            vv = jnp.broadcast_to(column, (NR, 2 * LANES))
            w_ref[u] = (psi * jnp.concatenate([vv, vv], axis=0)).astype(BF)
        for u in range(batch):
            m = jnp.dot(ix_ref[...], w_ref[u], preferred_element_type=F32)
            rows = pl.ds(pl.multiple_of((i * batch + u) * tall, 8), tall)
            for h in range(2):
                s_ref[h, rows, :] = m[:, h * LANES : (h + 1) * LANES]

    @pl.loop(0, SIDE // turn)
    def _(i):
        xs = []
        for u in range(turn):
            rows = pl.ds(i * turn + u, 2 * NR, stride=BOX)
            xs.append(jnp.concatenate([s_ref[h, rows, :].astype(BF) for h in range(2)], axis=1))
        for u in range(turn):
            m = jnp.dot(iy_ref[...], xs[u], preferred_element_type=F32)
            r0 = (i * turn + u) * 4 * BOX
            for h in range(2):
                for p in range(2):
                    g_ref[pl.ds(r0 + 2 * h + p, BOX, stride=4), :] = m[
                        p * BOX : (p + 1) * BOX, h * LANES : (h + 1) * LANES
                    ]

    for q in range(PIECES):

        @pl.loop(q * sticks // PIECES // step, (q + 1) * sticks // PIECES // step)
        def _(i):
            for u in range(step):
                c = cell_ref[i * step + u]
                f_ref[pl.ds(pl.multiple_of(i * 4 * step, 4 * step) + 4 * u, 4), :] = g_ref[
                    pl.ds(pl.multiple_of(4 * c, 4), 4), :
                ]

        @pl.loop(q * share // 4, (q + 1) * share // 4)
        def _(i):
            for u in range(4):
                o = i * 4 + u
                o_ref[o] = f_ref[pl.ds(pl.multiple_of(o * PER, PER), PER), :].astype(BF)


def plane_pass(cells, received, volume, tabs):
    owners = received.shape[0]
    return pl.pallas_call(
        plane_kernel,
        out_shape=jax.ShapeDtypeStruct((owners, PER, LANES), BF),
        in_specs=[SMEM, VMEM] + [HBM] * 5,
        out_specs=VMEM,
        scratch_shapes=[
            pltpu.VMEM(volume.shape, F32),
            *[pltpu.VMEM(t.shape, BF) for t in tabs],
            pltpu.VMEM((owners * PER, LANES), F32),
            pltpu.VMEM((SIDE * BOX * 4, LANES), F32),
            pltpu.VMEM((2, 2 * NR * BOX, LANES), F32),
            pltpu.VMEM((16, 2 * NR, 2 * LANES), BF),
            pltpu.SemaphoreType.DMA((5,)),
        ],
        compiler_params=pltpu.CompilerParams(vmem_limit_bytes=42 << 20),
        cost_estimate=pl.CostEstimate(
            flops=2 * 77000 * 256 * 256, bytes_accessed=6 << 20, transcendentals=0
        ),
        name="plane",
    )(cells, received, volume, *tabs)


def finish_kernel(r_ref, place_ref, i_ref, o_hbm, t_ref, sp_ref, out_ref, sem):
    place = place_ref[...]
    count = place.shape[1]
    spot = ((place >> 7) * BOX + ((place + HALF) & (NR - 1))).astype(F32)
    across = lax.broadcasted_iota(jnp.int32, (count, count), 1)
    down = lax.broadcasted_iota(jnp.int32, (count, count), 0)
    row = jnp.sum(jnp.where(across == down, spot, 0.0), axis=1, keepdims=True).astype(jnp.int32)
    at = lax.broadcasted_iota(jnp.int32, (count, SLOT * BOX), 1)
    select = jnp.where(at == row, 1.0 / NR**3, 0.0).astype(BF)

    @pl.loop(0, NR // 4)
    def _(i):
        for u in range(4):
            k = i * 4 + u
            t_ref[pl.ds(pl.multiple_of(k * PER, PER), PER), :] = r_ref[k].astype(F32)

    for s in range(SLOT):
        halves = [
            jnp.concatenate(
                [t_ref[pl.ds(4 * s + 2 * h + p, NR, stride=PER), :] for p in range(2)], axis=0
            )
            for h in range(2)
        ]
        x = jnp.concatenate(halves, axis=1).astype(BF)
        m = jnp.dot(i_ref[...], x, preferred_element_type=F32)
        for p in range(2):
            sp_ref[p, s * BOX : (s + 1) * BOX, :] = m[p * BOX : (p + 1) * BOX]
    sends = []
    for p in range(2):
        out_ref[p] = jnp.dot(select, sp_ref[p].astype(BF), preferred_element_type=F32)
        sends.append(pltpu.make_async_copy(out_ref.at[p], o_hbm.at[p], sem.at[p]))
        sends[p].start()
    for copy in sends:
        copy.wait()


def finish(returned, place, behind_z):
    out = jax.ShapeDtypeStruct((2, place.shape[1], 2 * LANES), F32)
    return pl.pallas_call(
        finish_kernel,
        out_shape=out,
        in_specs=[VMEM] * 3,
        out_specs=HBM,
        scratch_shapes=[
            pltpu.VMEM((NR * PER, LANES), F32),
            pltpu.VMEM((2, SLOT * BOX, 2 * LANES), F32),
            pltpu.VMEM(out.shape, F32),
            pltpu.SemaphoreType.DMA((2,)),
        ],
        compiler_params=pltpu.CompilerParams(vmem_limit_bytes=24 << 20),
        cost_estimate=pl.CostEstimate(
            flops=2 * (2304 + 2560) * 256 * 256, bytes_accessed=3 << 20, transcendentals=0
        ),
        name="finish",
    )(returned, place, behind_z)


def exchange(value):
    return lax.all_to_all(value, TG_PW, split_axis=0, concat_axis=0, tiled=True)


def body(coeffs, g_place, stick_column, potential):
    ahead_x, behind_x, behind_y, ahead_y = tables()
    place = g_place.reshape(1, -1)
    sent = spread(coeffs, place, stick_column, ahead_x)
    got = exchange(sent)
    column = got[:, PER, : 2 * SLOT].astype(F32).astype(jnp.int32)
    cells = (column[:, :SLOT] * BOX + column[:, SLOT:]).reshape(-1)
    volume = potential.reshape(NR, NR)
    done = plane_pass(cells, got, volume, (ahead_y, ahead_x, behind_x, behind_y))
    return finish(exchange(done), place, behind_x)


def solution(mesh):
    torus = Mesh(mesh.devices.reshape(mesh.shape["tg"], 4, 4, 4), ("tg", "pw_0", "pw_1", "pw_2"))
    return jax.shard_map(
        body,
        mesh=torus,
        in_specs=(P(None, TG_PW, None), P(TG_PW), P(TG_PW), P(None, None, TG_PW)),
        out_specs=P(None, TG_PW, None),
        check_vma=False,
    )
```

time: 116 us -> 113 us (0.974)
  blocking collectives: 0 us -> 78.3 us
  starting transfers between devices: 34.9 us -> 0 us
  waiting for transfers between devices: 33 us -> 0 us
  Pallas kernels: 46.3 us -> 34.6 us
    all_to_all x0 -> x2, blocking collectives: none -> 78.3 us  [exchange(): return lax.all_to_all(value, TG_PW, split_axis=0, concat_axis=0, tiled=True)]
    all_to_all x4 -> x0, starting transfers between devices: 34.9 us -> none  [exchange(): return lax.all_to_all(value, TG_PW, split_axis=0, concat_axis=0, tiled=True)]
    all_to_all x4 -> x0, waiting for transfers between devices: 33 us -> none  [exchange(): return lax.all_to_all(value, TG_PW, split_axis=0, concat_axis=0, tiled=True)]
    pallas_call x6 -> x3, Pallas kernels: 46.3 us -> 34.6 us  [the longest x1 24.1 us: plane_pass(): pl.pallas_call(plane_kernel, out_shape=jax.ShapeDtypeStruct((owners, PER,...]
  transfers between devices with their start and end apart: 4 -> 0, of which waited for: 4 -> 0; matrix products, arithmetic and copies ran while one was open for 1% -> 0% of each run, Pallas kernels for 34% -> 0%
where the time goes in v2:
time: 113 us
  blocking collectives  78.3 us (69%)
  Pallas kernels  34.6 us (31%)
    all_to_all x2, blocking collectives, exchange(): return lax.all_to_all(value, TG_PW, split_axis=0, concat_axis=0, tiled=True)  78.3 us
    pallas_call x1, Pallas kernels, plane_pass(): pl.pallas_call(plane_kernel, out_shape=jax.ShapeDtypeStruct((owners, PER,...  24.1 us
    pallas_call x1, Pallas kernels, spread(): pl.pallas_call(spread_kernel, out_shape=out, in_specs=[HBM, HBM, SMEM, HB...  6.27 us
    pallas_call x1, Pallas kernels, finish(): pl.pallas_call(finish_kernel, out_shape=out, in_specs=[VMEM] * 3, out_spe...  4.2 us

profile of v2, /device:TPU:1, one launch (start us, length us, event | category | flops | bytes accessed | tf_op | source)
XLA Modules:
  0.0 113.2 jit_solution(4183651059211146074)
XLA Ops:
  0.0 6.3 %spread.1 = bf16[128,72,128]{2,1,0:T(8,128)(2,1)} custom-call(f32[2,256,256]{2,1,0:T(8,128)} %c_hbm.1, s32[1,256]{1,0:T(1,128)} %bitcast.3, s32[16]{0:T(128)} %column_ref.1, bf16[256,144]{1,0:T(8,128)(2,1)} %constant.10.clone.e_hbm.ex_hbm), custom_call_target="tpu_custom_call" | custom-call | flops 838860800 | bytes 3145728 | tf_op jit(solution)/shard_map/spread/pallas_call | solution.py:110
  6.3 0.0 copy-start
  6.3 0.0 copy-start.2
  6.3 0.0 copy-start.3
  6.3 0.0 copy-start.4
  6.3 0.0 copy-start.5
  6.3 42.9 %all_to_all.10.r_in = bf16[128,72,128]{2,1,0:T(8,128)(2,1)S(1)} all-to-all(bf16[128,72,128]{2,1,0:T(8,128)(2,1)} %spread.1), channel_id=1, replica_groups=mesh['tg'=2,'pw_0'=4,'pw_1'=4,'pw_2'=4] {'tg','pw_0','pw_1','pw_2'}, dimensions={0} | all-to-all | bytes 4718592 | tf_op jit(solution)/shard_map/all_to_all | solution.py:338
  49.2 0.1 fusion
  49.3 0.1 slice_add_fusion
  49.3 0.1 reshape.12.cell_ref
  49.4 0.0 copy-done
  49.4 0.0 copy-done.2
  49.4 0.0 copy-done.3
  49.5 0.0 copy-done.4
  49.5 0.0 copy-done.5
  49.5 24.1 %plane.1 = bf16[128,64,128]{2,1,0:T(8,128)(2,1)S(1)} custom-call(s32[2048]{0:T(1024)S(1)} %reshape.12.cell_ref, bf16[128,72,128]{2,1,0:T(8,128)(2,1)S(1)} %all_to_all.10.r_in, f32[128,128]{1,0:T(8,128)S(1)} %bitcast.5, bf16[256,144]{1,0:T(8,128)(2,1)S(1)} %copy-done.4, bf16[256,144]{1,0:T(8,128)(2,1)S(1)} %copy-done.3, bf16[144,256]{1,0:T(8,128)(2,1)S(1)} %copy-done, ...), custom_call_target="tpu_custom_call" | custom-call | flops 10092544000 | bytes 6291456 | tf_op jit(solution)/shard_map/plane/pallas_call | solution.py:258
  73.6 0.0 copy-start.1
  73.6 35.4 %all_to_all.11.r_ref = bf16[128,64,128]{2,1,0:T(8,128)(2,1)S(1)} all-to-all(bf16[128,64,128]{2,1,0:T(8,128)(2,1)S(1)} %plane.1), channel_id=1, replica_groups=mesh['tg'=2,'pw_0'=4,'pw_1'=4,'pw_2'=4] {'tg','pw_0','pw_1','pw_2'}, dimensions={0} | all-to-all | bytes 4194304 | tf_op jit(solution)/shard_map/all_to_all | solution.py:338
  109.0 0.0 copy-done.1
  109.0 4.2 %finish.1 = f32[2,256,256]{2,1,0:T(8,128)} custom-call(bf16[128,64,128]{2,1,0:T(8,128)(2,1)S(1)} %all_to_all.11.r_ref, s32[1,256]{1,0:T(1,128)S(1)} %bitcast.4, bf16[144,256]{1,0:T(8,128)(2,1)S(1)} %copy-done), custom_call_target="tpu_custom_call" | custom-call | flops 637534208 | bytes 3145728 | tf_op jit(solution)/shard_map/finish/pallas_call | solution.py:318
Async XLA Ops:
  6.3 43.2 %copy-start = (bf16[144,256]{1,0:T(8,128)(2,1)S(1)}, bf16[144,256]{1,0:T(8,128)(2,1)}, u32[]{:S(2)}) copy-start(bf16[144,256]{1,0:T(8,128)(2,1)} %constant.11.clone.ix_hbm.i_ref) | copy-start | bytes 221188
  6.3 43.1 %copy-start.2 = (f32[128,128,1]{1,2,0:T(1,128)S(1)}, f32[128,128,1]{1,2,0:T(1,128)}, u32[]{:S(2)}) copy-start(f32[128,128,1]{1,2,0:T(1,128)} %param.11) | copy-start | bytes 196612
  6.3 43.1 %copy-start.3 = (bf16[256,144]{1,0:T(8,128)(2,1)S(1)}, bf16[256,144]{1,0:T(8,128)(2,1)}, u32[]{:S(2)}) copy-start(bf16[256,144]{1,0:T(8,128)(2,1)} %constant.10.clone.e_hbm.ex_hbm) | copy-start | bytes 221188
  6.3 43.1 %copy-start.4 = (bf16[256,144]{1,0:T(8,128)(2,1)S(1)}, bf16[256,144]{1,0:T(8,128)(2,1)}, u32[]{:S(2)}) copy-start(bf16[256,144]{1,0:T(8,128)(2,1)} %constant.13.clone.ey_hbm) | copy-start | bytes 221188
  6.3 43.1 %copy-start.5 = (bf16[144,256]{1,0:T(8,128)(2,1)S(1)}, bf16[144,256]{1,0:T(8,128)(2,1)}, u32[]{:S(2)}) copy-start(bf16[144,256]{1,0:T(8,128)(2,1)} %constant.12.clone.iy_hbm) | copy-start | bytes 221188
  73.6 35.4 %copy-start.1 = (s32[256]{0:T(256)S(1)}, s32[256]{0:T(256)}, u32[]{:S(2)}) copy-start(s32[256]{0:T(256)} %param.9) | copy-start | bytes 3076

commit v3 on v2

--- a/solution.py
+++ b/solution.py
@@ -13,9 +13,11 @@
 HALF = 32
 BOX = 72
 SIDE = 65
+STEP = 73
 SLOT = 16
 LANES = 128
 PER = 4 * SLOT
+WIDE = PER + 1
 PIECES = 4
 TG_PW = ("tg", "pw_0", "pw_1", "pw_2")
 BF = jnp.bfloat16
@@ -83,19 +85,18 @@
         m = jnp.dot(e_ref[...], xs[s], preferred_element_type=F32)
         for h in range(2):
             for p in range(2):
-                t_ref[pl.ds(4 * s + 2 * h + p, NR, stride=PER), :] = m[
+                t_ref[pl.ds(4 * s + 2 * h + p, NR, stride=WIDE), :] = m[
                     p * NR : (p + 1) * NR, h * LANES : (h + 1) * LANES
                 ]
     share = NR // PIECES
     sends = []
     for q in range(PIECES):
 
-        @pl.loop(q * share // 4, (q + 1) * share // 4)
-        def _(i):
-            for u in range(4):
-                k = i * 4 + u
-                rows = pl.ds(pl.multiple_of(k * PER, PER), PER)
-                o_ref[k, 0:PER, :] = t_ref[rows, :].astype(BF)
+        @pl.loop(q * share // 8, (q + 1) * share // 8)
+        def _(i):
+            for u in range(8):
+                k = i * 8 + u
+                o_ref[k, 0:PER, :] = t_ref[pl.ds(k * WIDE, PER), :].astype(BF)
                 o_ref[k, PER : PER + 8, :] = info
 
         part = pl.ds(q * share, share)
@@ -116,7 +117,7 @@
             pltpu.VMEM(coeffs.shape, F32),
             pltpu.VMEM(place.shape, jnp.int32),
             pltpu.VMEM(ahead_z.shape, BF),
-            pltpu.VMEM((NR * PER, LANES), F32),
+            pltpu.VMEM((NR * WIDE, LANES), F32),
             pltpu.VMEM(out.shape, BF),
             pltpu.SemaphoreType.DMA((PIECES + 1,)),
         ],
@@ -134,7 +135,6 @@
 ):
     owners = o_ref.shape[0]
     sticks = owners * SLOT
-    tall = 2 * BOX
     share = owners // PIECES
     fixed = [
         pltpu.make_async_copy(src, dst, sem.at[n])
@@ -154,7 +154,7 @@
     def _(i):
         for u in range(16):
             for h in range(2):
-                s_ref[h, pl.ds(pl.multiple_of((i * 16 + u) * BOX + 64, 8), 8), :] = blank[:8]
+                s_ref[h, pl.ds((i * 16 + u) * STEP + 64, 8), :] = blank[:8]
 
     step = 32
     for q in range(PIECES):
@@ -194,7 +194,7 @@
         for u in range(turn):
             m = jnp.dot(ey_ref[...], xs[u], preferred_element_type=F32)
             for h in range(2):
-                s_ref[h, pl.ds(i * turn + u, 2 * NR, stride=BOX), :] = m[
+                s_ref[h, pl.ds(i * turn + u, 2 * NR, stride=STEP), :] = m[
                     :, h * LANES : (h + 1) * LANES
                 ]
 
@@ -206,8 +206,14 @@
     def _(i):
         xs = []
         for u in range(batch):
-            rows = pl.ds(pl.multiple_of((i * batch + u) * tall, 8), tall)
-            xs.append(jnp.concatenate([s_ref[h, rows, :].astype(BF) for h in range(2)], axis=1))
+            r0 = (i * batch + u) * 2 * STEP
+            halves = [
+                jnp.concatenate(
+                    [s_ref[h, pl.ds(r0 + p * STEP, BOX), :] for p in range(2)], axis=0
+                )
+                for h in range(2)
+            ]
+            xs.append(jnp.concatenate(halves, axis=1).astype(BF))
         for u in range(batch):
             psi = jnp.dot(ex_ref[...], xs[u], preferred_element_type=F32)
             column = jnp.sum(
@@ -217,15 +223,18 @@
             w_ref[u] = (psi * jnp.concatenate([vv, vv], axis=0)).astype(BF)
         for u in range(batch):
             m = jnp.dot(ix_ref[...], w_ref[u], preferred_element_type=F32)
-            rows = pl.ds(pl.multiple_of((i * batch + u) * tall, 8), tall)
+            r0 = (i * batch + u) * 2 * STEP
             for h in range(2):
-                s_ref[h, rows, :] = m[:, h * LANES : (h + 1) * LANES]
+                for p in range(2):
+                    s_ref[h, pl.ds(r0 + p * STEP, BOX), :] = m[
+                        p * BOX : (p + 1) * BOX, h * LANES : (h + 1) * LANES
+                    ]
 
     @pl.loop(0, SIDE // turn)
     def _(i):
         xs = []
         for u in range(turn):
-            rows = pl.ds(i * turn + u, 2 * NR, stride=BOX)
+            rows = pl.ds(i * turn + u, 2 * NR, stride=STEP)
             xs.append(jnp.concatenate([s_ref[h, rows, :].astype(BF) for h in range(2)], axis=1))
         for u in range(turn):
             m = jnp.dot(iy_ref[...], xs[u], preferred_element_type=F32)
@@ -265,7 +274,7 @@
             *[pltpu.VMEM(t.shape, BF) for t in tabs],
             pltpu.VMEM((owners * PER, LANES), F32),
             pltpu.VMEM((SIDE * BOX * 4, LANES), F32),
-            pltpu.VMEM((2, 2 * NR * BOX, LANES), F32),
+            pltpu.VMEM((2, 2 * NR * STEP, LANES), F32),
             pltpu.VMEM((16, 2 * NR, 2 * LANES), BF),
             pltpu.SemaphoreType.DMA((5,)),
         ],
@@ -287,16 +296,16 @@
     at = lax.broadcasted_iota(jnp.int32, (count, SLOT * BOX), 1)
     select = jnp.where(at == row, 1.0 / NR**3, 0.0).astype(BF)
 
-    @pl.loop(0, NR // 4)
-    def _(i):
-        for u in range(4):
-            k = i * 4 + u
-            t_ref[pl.ds(pl.multiple_of(k * PER, PER), PER), :] = r_ref[k].astype(F32)
+    @pl.loop(0, NR // 8)
+    def _(i):
+        for u in range(8):
+            k = i * 8 + u
+            t_ref[pl.ds(k * WIDE, PER), :] = r_ref[k].astype(F32)
 
     for s in range(SLOT):
         halves = [
             jnp.concatenate(
-                [t_ref[pl.ds(4 * s + 2 * h + p, NR, stride=PER), :] for p in range(2)], axis=0
+                [t_ref[pl.ds(4 * s + 2 * h + p, NR, stride=WIDE), :] for p in range(2)], axis=0
             )
             for h in range(2)
         ]
@@ -321,7 +330,7 @@
         in_specs=[VMEM] * 3,
         out_specs=HBM,
         scratch_shapes=[
-            pltpu.VMEM((NR * PER, LANES), F32),
+            pltpu.VMEM((NR * WIDE, LANES), F32),
             pltpu.VMEM((2, SLOT * BOX, 2 * LANES), F32),
             pltpu.VMEM(out.shape, F32),
             pltpu.SemaphoreType.DMA((2,)),

time: 113 us -> 106 us (0.938)
  Pallas kernels: 34.6 us -> 27.5 us
    pallas_call x1, Pallas kernels: 24.1 us -> 21 us  [plane_pass(): pl.pallas_call(plane_kernel, out_shape=jax.ShapeDtypeStruct((owners, PER,...]
    pallas_call x1, Pallas kernels: 4.2 us -> 2.16 us  [finish(): pl.pallas_call(finish_kernel, out_shape=out, in_specs=[VMEM] * 3, out_spe...]
    pallas_call x1, Pallas kernels: 6.27 us -> 4.28 us  [spread(): pl.pallas_call(spread_kernel, out_shape=out, in_specs=[HBM, HBM, SMEM, HB...]
where the time goes in v3:
time: 106 us
  blocking collectives  78.3 us (74%)
  Pallas kernels  27.5 us (26%)
    all_to_all x2, blocking collectives, exchange(): return lax.all_to_all(value, TG_PW, split_axis=0, concat_axis=0, tiled=True)  78.3 us
    pallas_call x1, Pallas kernels, plane_pass(): pl.pallas_call(plane_kernel, out_shape=jax.ShapeDtypeStruct((owners, PER,...  21 us
    pallas_call x1, Pallas kernels, spread(): pl.pallas_call(spread_kernel, out_shape=out, in_specs=[HBM, HBM, SMEM, HB...  4.28 us
    pallas_call x1, Pallas kernels, finish(): pl.pallas_call(finish_kernel, out_shape=out, in_specs=[VMEM] * 3, out_spe...  2.16 us

profile of v3, /device:TPU:1, one launch (start us, length us, event | category | flops | bytes accessed | tf_op | source)
XLA Modules:
  0.0 106.1 jit_solution(5074439659355869392)
XLA Ops:
  0.0 4.3 %spread.1 = bf16[128,72,128]{2,1,0:T(8,128)(2,1)} custom-call(f32[2,256,256]{2,1,0:T(8,128)} %c_hbm.1, s32[1,256]{1,0:T(1,128)} %bitcast.3, s32[16]{0:T(128)} %column_ref.1, bf16[256,144]{1,0:T(8,128)(2,1)} %constant.10.clone.e_hbm.ex_hbm), custom_call_target="tpu_custom_call" | custom-call | flops 838860800 | bytes 3145728 | tf_op jit(solution)/shard_map/spread/pallas_call | solution.py:111
  4.3 0.0 copy-start
  4.3 0.0 copy-start.2
  4.3 0.0 copy-start.3
  4.3 0.0 copy-start.4
  4.3 0.0 copy-start.5
  4.3 42.9 %all_to_all.10.r_in = bf16[128,72,128]{2,1,0:T(8,128)(2,1)S(1)} all-to-all(bf16[128,72,128]{2,1,0:T(8,128)(2,1)} %spread.1), channel_id=1, replica_groups=mesh['tg'=2,'pw_0'=4,'pw_1'=4,'pw_2'=4] {'tg','pw_0','pw_1','pw_2'}, dimensions={0} | all-to-all | bytes 4718592 | tf_op jit(solution)/shard_map/all_to_all | solution.py:347
  47.2 0.1 fusion
  47.3 0.1 slice_add_fusion
  47.4 0.1 reshape.12.cell_ref
  47.4 0.0 copy-done
  47.4 0.0 copy-done.2
  47.5 0.0 copy-done.3
  47.5 0.0 copy-done.4
  47.5 0.0 copy-done.5
  47.5 21.0 %plane.1 = bf16[128,64,128]{2,1,0:T(8,128)(2,1)S(1)} custom-call(s32[2048]{0:T(1024)S(1)} %reshape.12.cell_ref, bf16[128,72,128]{2,1,0:T(8,128)(2,1)S(1)} %all_to_all.10.r_in, f32[128,128]{1,0:T(8,128)S(1)} %bitcast.5, bf16[256,144]{1,0:T(8,128)(2,1)S(1)} %copy-done.4, bf16[256,144]{1,0:T(8,128)(2,1)S(1)} %copy-done.3, bf16[144,256]{1,0:T(8,128)(2,1)S(1)} %copy-done, ...), custom_call_target="tpu_custom_call" | custom-call | flops 10092544000 | bytes 6291456 | tf_op jit(solution)/shard_map/plane/pallas_call | solution.py:267
  68.5 0.0 copy-start.1
  68.5 35.4 %all_to_all.11.r_ref = bf16[128,64,128]{2,1,0:T(8,128)(2,1)S(1)} all-to-all(bf16[128,64,128]{2,1,0:T(8,128)(2,1)S(1)} %plane.1), channel_id=1, replica_groups=mesh['tg'=2,'pw_0'=4,'pw_1'=4,'pw_2'=4] {'tg','pw_0','pw_1','pw_2'}, dimensions={0} | all-to-all | bytes 4194304 | tf_op jit(solution)/shard_map/all_to_all | solution.py:347
  103.9 0.0 copy-done.1
  103.9 2.2 %finish.1 = f32[2,256,256]{2,1,0:T(8,128)} custom-call(bf16[128,64,128]{2,1,0:T(8,128)(2,1)S(1)} %all_to_all.11.r_ref, s32[1,256]{1,0:T(1,128)S(1)} %bitcast.4, bf16[144,256]{1,0:T(8,128)(2,1)S(1)} %copy-done), custom_call_target="tpu_custom_call" | custom-call | flops 637534208 | bytes 3145728 | tf_op jit(solution)/shard_map/finish/pallas_call | solution.py:327
Async XLA Ops:
  4.3 43.2 %copy-start = (bf16[144,256]{1,0:T(8,128)(2,1)S(1)}, bf16[144,256]{1,0:T(8,128)(2,1)}, u32[]{:S(2)}) copy-start(bf16[144,256]{1,0:T(8,128)(2,1)} %constant.11.clone.ix_hbm.i_ref) | copy-start | bytes 221188
  4.3 43.1 %copy-start.2 = (f32[128,128,1]{1,2,0:T(1,128)S(1)}, f32[128,128,1]{1,2,0:T(1,128)}, u32[]{:S(2)}) copy-start(f32[128,128,1]{1,2,0:T(1,128)} %param.11) | copy-start | bytes 196612
  4.3 43.1 %copy-start.3 = (bf16[256,144]{1,0:T(8,128)(2,1)S(1)}, bf16[256,144]{1,0:T(8,128)(2,1)}, u32[]{:S(2)}) copy-start(bf16[256,144]{1,0:T(8,128)(2,1)} %constant.10.clone.e_hbm.ex_hbm) | copy-start | bytes 221188
  4.3 43.1 %copy-start.4 = (bf16[256,144]{1,0:T(8,128)(2,1)S(1)}, bf16[256,144]{1,0:T(8,128)(2,1)}, u32[]{:S(2)}) copy-start(bf16[256,144]{1,0:T(8,128)(2,1)} %constant.13.clone.ey_hbm) | copy-start | bytes 221188
  4.3 43.1 %copy-start.5 = (bf16[144,256]{1,0:T(8,128)(2,1)S(1)}, bf16[144,256]{1,0:T(8,128)(2,1)}, u32[]{:S(2)}) copy-start(bf16[144,256]{1,0:T(8,128)(2,1)} %constant.12.clone.iy_hbm) | copy-start | bytes 221188
  68.5 35.4 %copy-start.1 = (s32[256]{0:T(256)S(1)}, s32[256]{0:T(256)}, u32[]{:S(2)}) copy-start(s32[256]{0:T(256)} %param.9) | copy-start | bytes 3076

commit v4 on v3

--- a/solution.py
+++ b/solution.py
@@ -156,13 +156,13 @@
             for h in range(2):
                 s_ref[h, pl.ds((i * 16 + u) * STEP + 64, 8), :] = blank[:8]
 
-    step = 32
+    step = 128
     for q in range(PIECES):
 
-        @pl.loop(q * share // 4, (q + 1) * share // 4)
-        def _(i):
-            for u in range(4):
-                o = i * 4 + u
+        @pl.loop(q * share // 16, (q + 1) * share // 16)
+        def _(i):
+            for u in range(16):
+                o = i * 16 + u
                 f_ref[pl.ds(pl.multiple_of(o * PER, PER), PER), :] = r_in[
                     o, 0:PER, :
                 ].astype(F32)
@@ -177,7 +177,7 @@
 
     for copy in fixed:
         copy.wait()
-    turn = 13
+    turn = SIDE
 
     @pl.loop(0, SIDE // turn)
     def _(i):
@@ -200,7 +200,7 @@
 
     lane = lax.broadcasted_iota(jnp.int32, (NR, NR), 1)
     v = v_ref[...]
-    batch = 16
+    batch = 32
 
     @pl.loop(0, NR // batch)
     def _(i):
@@ -255,10 +255,10 @@
                     pl.ds(pl.multiple_of(4 * c, 4), 4), :
                 ]
 
-        @pl.loop(q * share // 4, (q + 1) * share // 4)
-        def _(i):
-            for u in range(4):
-                o = i * 4 + u
+        @pl.loop(q * share // 16, (q + 1) * share // 16)
+        def _(i):
+            for u in range(16):
+                o = i * 16 + u
                 o_ref[o] = f_ref[pl.ds(pl.multiple_of(o * PER, PER), PER), :].astype(BF)
 
 
@@ -275,10 +275,10 @@
             pltpu.VMEM((owners * PER, LANES), F32),
             pltpu.VMEM((SIDE * BOX * 4, LANES), F32),
             pltpu.VMEM((2, 2 * NR * STEP, LANES), F32),
-            pltpu.VMEM((16, 2 * NR, 2 * LANES), BF),
+            pltpu.VMEM((32, 2 * NR, 2 * LANES), BF),
             pltpu.SemaphoreType.DMA((5,)),
         ],
-        compiler_params=pltpu.CompilerParams(vmem_limit_bytes=42 << 20),
+        compiler_params=pltpu.CompilerParams(vmem_limit_bytes=48 << 20),
         cost_estimate=pl.CostEstimate(
             flops=2 * 77000 * 256 * 256, bytes_accessed=6 << 20, transcendentals=0
         ),

time: 106 us -> 104 us (0.981)
  Pallas kernels: 27.5 us -> 25.1 us
    pallas_call x1, Pallas kernels: 21 us -> 18.6 us  [plane_pass(): pl.pallas_call(plane_kernel, out_shape=jax.ShapeDtypeStruct((owners, PER,...]
where the time goes in v4:
time: 104 us
  blocking collectives  78.3 us (75%)
  Pallas kernels  25.1 us (24%)
    all_to_all x2, blocking collectives, exchange(): return lax.all_to_all(value, TG_PW, split_axis=0, concat_axis=0, tiled=True)  78.3 us
    pallas_call x1, Pallas kernels, plane_pass(): pl.pallas_call(plane_kernel, out_shape=jax.ShapeDtypeStruct((owners, PER,...  18.6 us
    pallas_call x1, Pallas kernels, spread(): pl.pallas_call(spread_kernel, out_shape=out, in_specs=[HBM, HBM, SMEM, HB...  4.28 us
    pallas_call x1, Pallas kernels, finish(): pl.pallas_call(finish_kernel, out_shape=out, in_specs=[VMEM] * 3, out_spe...  2.16 us

profile of v4, /device:TPU:1, one launch (start us, length us, event | category | flops | bytes accessed | tf_op | source)
XLA Modules:
  0.0 103.7 jit_solution(10681437752059878029)
XLA Ops:
  0.0 4.3 %spread.1 = bf16[128,72,128]{2,1,0:T(8,128)(2,1)} custom-call(f32[2,256,256]{2,1,0:T(8,128)} %c_hbm.1, s32[1,256]{1,0:T(1,128)} %bitcast.3, s32[16]{0:T(128)} %column_ref.1, bf16[256,144]{1,0:T(8,128)(2,1)} %constant.10.clone.e_hbm.ex_hbm), custom_call_target="tpu_custom_call" | custom-call | flops 838860800 | bytes 3145728 | tf_op jit(solution)/shard_map/spread/pallas_call | solution.py:111
  4.3 0.0 copy-start
  4.3 0.0 copy-start.2
  4.3 0.0 copy-start.3
  4.3 0.0 copy-start.4
  4.3 0.0 copy-start.5
  4.3 42.9 %all_to_all.10.r_in = bf16[128,72,128]{2,1,0:T(8,128)(2,1)S(1)} all-to-all(bf16[128,72,128]{2,1,0:T(8,128)(2,1)} %spread.1), channel_id=1, replica_groups=mesh['tg'=2,'pw_0'=4,'pw_1'=4,'pw_2'=4] {'tg','pw_0','pw_1','pw_2'}, dimensions={0} | all-to-all | bytes 4718592 | tf_op jit(solution)/shard_map/all_to_all | solution.py:347
  47.2 0.1 fusion
  47.3 0.1 slice_add_fusion
  47.4 0.1 reshape.12.cell_ref
  47.4 0.0 copy-done
  47.4 0.0 copy-done.2
  47.5 0.0 copy-done.3
  47.5 0.0 copy-done.4
  47.5 0.0 copy-done.5
  47.5 18.6 %plane.1 = bf16[128,64,128]{2,1,0:T(8,128)(2,1)S(1)} custom-call(s32[2048]{0:T(1024)S(1)} %reshape.12.cell_ref, bf16[128,72,128]{2,1,0:T(8,128)(2,1)S(1)} %all_to_all.10.r_in, f32[128,128]{1,0:T(8,128)S(1)} %bitcast.5, bf16[256,144]{1,0:T(8,128)(2,1)S(1)} %copy-done.4, bf16[256,144]{1,0:T(8,128)(2,1)S(1)} %copy-done.3, bf16[144,256]{1,0:T(8,128)(2,1)S(1)} %copy-done, ...), custom_call_target="tpu_custom_call" | custom-call | flops 10092544000 | bytes 6291456 | tf_op jit(solution)/shard_map/plane/pallas_call | solution.py:267
  66.1 0.0 copy-start.1
  66.1 35.4 %all_to_all.11.r_ref = bf16[128,64,128]{2,1,0:T(8,128)(2,1)S(1)} all-to-all(bf16[128,64,128]{2,1,0:T(8,128)(2,1)S(1)} %plane.1), channel_id=1, replica_groups=mesh['tg'=2,'pw_0'=4,'pw_1'=4,'pw_2'=4] {'tg','pw_0','pw_1','pw_2'}, dimensions={0} | all-to-all | bytes 4194304 | tf_op jit(solution)/shard_map/all_to_all | solution.py:347
  101.5 0.0 copy-done.1
  101.5 2.2 %finish.1 = f32[2,256,256]{2,1,0:T(8,128)} custom-call(bf16[128,64,128]{2,1,0:T(8,128)(2,1)S(1)} %all_to_all.11.r_ref, s32[1,256]{1,0:T(1,128)S(1)} %bitcast.4, bf16[144,256]{1,0:T(8,128)(2,1)S(1)} %copy-done), custom_call_target="tpu_custom_call" | custom-call | flops 637534208 | bytes 3145728 | tf_op jit(solution)/shard_map/finish/pallas_call | solution.py:327
Async XLA Ops:
  4.3 43.2 %copy-start = (bf16[144,256]{1,0:T(8,128)(2,1)S(1)}, bf16[144,256]{1,0:T(8,128)(2,1)}, u32[]{:S(2)}) copy-start(bf16[144,256]{1,0:T(8,128)(2,1)} %constant.11.clone.ix_hbm.i_ref) | copy-start | bytes 221188
  4.3 43.1 %copy-start.2 = (f32[128,128,1]{1,2,0:T(1,128)S(1)}, f32[128,128,1]{1,2,0:T(1,128)}, u32[]{:S(2)}) copy-start(f32[128,128,1]{1,2,0:T(1,128)} %param.11) | copy-start | bytes 196612
  4.3 43.1 %copy-start.3 = (bf16[256,144]{1,0:T(8,128)(2,1)S(1)}, bf16[256,144]{1,0:T(8,128)(2,1)}, u32[]{:S(2)}) copy-start(bf16[256,144]{1,0:T(8,128)(2,1)} %constant.10.clone.e_hbm.ex_hbm) | copy-start | bytes 221188
  4.3 43.1 %copy-start.4 = (bf16[256,144]{1,0:T(8,128)(2,1)S(1)}, bf16[256,144]{1,0:T(8,128)(2,1)}, u32[]{:S(2)}) copy-start(bf16[256,144]{1,0:T(8,128)(2,1)} %constant.13.clone.ey_hbm) | copy-start | bytes 221188
  4.3 43.1 %copy-start.5 = (bf16[144,256]{1,0:T(8,128)(2,1)S(1)}, bf16[144,256]{1,0:T(8,128)(2,1)}, u32[]{:S(2)}) copy-start(bf16[144,256]{1,0:T(8,128)(2,1)} %constant.12.clone.iy_hbm) | copy-start | bytes 221188
  66.1 35.4 %copy-start.1 = (s32[256]{0:T(256)S(1)}, s32[256]{0:T(256)}, u32[]{:S(2)}) copy-start(s32[256]{0:T(256)} %param.9) | copy-start | bytes 3076

commit v5 on v4

--- a/solution.py
+++ b/solution.py
@@ -18,7 +18,7 @@
 LANES = 128
 PER = 4 * SLOT
 WIDE = PER + 1
-PIECES = 4
+PIECES = 8
 TG_PW = ("tg", "pw_0", "pw_1", "pw_2")
 BF = jnp.bfloat16
 F32 = jnp.float32
@@ -130,18 +130,20 @@
 
 
 def plane_kernel(
-    cell_ref, r_in, v_hbm, ey_hbm, ex_hbm, ix_hbm, iy_hbm, o_ref,
-    v_ref, ey_ref, ex_ref, ix_ref, iy_ref, f_ref, g_ref, s_ref, w_ref, sem,
+    r_in, v_hbm, ey_hbm, ex_hbm, ix_hbm, iy_hbm, o_ref,
+    v_ref, ey_ref, ex_ref, ix_ref, iy_ref, f_ref, g_ref, s_ref, w_ref, c_ref, cell_ref, sem,
 ):
     owners = o_ref.shape[0]
     sticks = owners * SLOT
-    share = owners // PIECES
     fixed = [
         pltpu.make_async_copy(src, dst, sem.at[n])
         for n, (src, dst) in enumerate(
             [(ey_hbm, ey_ref), (v_hbm, v_ref), (ex_hbm, ex_ref), (ix_hbm, ix_ref), (iy_hbm, iy_ref)]
         )
     ]
+    column = r_in[:, PER : PER + 8, :].astype(F32)[:, 0, :]
+    c_ref[...] = (column * BOX + pltpu.roll(column, LANES - SLOT, 1)).astype(jnp.int32)
+    index = pltpu.make_async_copy(c_ref, cell_ref, sem.at[5])
     for copy in fixed:
         copy.start()
     blank = jnp.zeros((4 * BOX, LANES), F32)
@@ -150,6 +152,8 @@
     def _(x):
         g_ref[pl.ds(pl.multiple_of(x * 4 * BOX, 8), 4 * BOX), :] = blank
 
+    index.start()
+
     @pl.loop(0, NR // 8)
     def _(i):
         for u in range(16):
@@ -157,23 +161,24 @@
                 s_ref[h, pl.ds((i * 16 + u) * STEP + 64, 8), :] = blank[:8]
 
     step = 128
-    for q in range(PIECES):
-
-        @pl.loop(q * share // 16, (q + 1) * share // 16)
-        def _(i):
-            for u in range(16):
-                o = i * 16 + u
-                f_ref[pl.ds(pl.multiple_of(o * PER, PER), PER), :] = r_in[
-                    o, 0:PER, :
-                ].astype(F32)
-
-        @pl.loop(q * sticks // PIECES // step, (q + 1) * sticks // PIECES // step)
-        def _(i):
-            for u in range(step):
-                c = cell_ref[i * step + u]
-                g_ref[pl.ds(pl.multiple_of(4 * c, 4), 4), :] = f_ref[
-                    pl.ds(pl.multiple_of(i * 4 * step, 4 * step) + 4 * u, 4), :
-                ]
+
+    @pl.loop(0, owners // 16)
+    def _(i):
+        for u in range(16):
+            o = i * 16 + u
+            f_ref[pl.ds(pl.multiple_of(o * PER, PER), PER), :] = r_in[
+                o, 0:PER, :
+            ].astype(F32)
+
+    index.wait()
+
+    @pl.loop(0, sticks // step)
+    def _(i):
+        for u in range(step):
+            c = cell_ref[i * (step // SLOT) + u // SLOT, u % SLOT]
+            g_ref[pl.ds(pl.multiple_of(4 * c, 4), 4), :] = f_ref[
+                pl.ds(pl.multiple_of(i * 4 * step, 4 * step) + 4 * u, 4), :
+            ]
 
     for copy in fixed:
         copy.wait()
@@ -245,29 +250,28 @@
                         p * BOX : (p + 1) * BOX, h * LANES : (h + 1) * LANES
                     ]
 
-    for q in range(PIECES):
-
-        @pl.loop(q * sticks // PIECES // step, (q + 1) * sticks // PIECES // step)
-        def _(i):
-            for u in range(step):
-                c = cell_ref[i * step + u]
-                f_ref[pl.ds(pl.multiple_of(i * 4 * step, 4 * step) + 4 * u, 4), :] = g_ref[
-                    pl.ds(pl.multiple_of(4 * c, 4), 4), :
-                ]
-
-        @pl.loop(q * share // 16, (q + 1) * share // 16)
-        def _(i):
-            for u in range(16):
-                o = i * 16 + u
-                o_ref[o] = f_ref[pl.ds(pl.multiple_of(o * PER, PER), PER), :].astype(BF)
-
-
-def plane_pass(cells, received, volume, tabs):
+
+    @pl.loop(0, sticks // step)
+    def _(i):
+        for u in range(step):
+            c = cell_ref[i * (step // SLOT) + u // SLOT, u % SLOT]
+            f_ref[pl.ds(pl.multiple_of(i * 4 * step, 4 * step) + 4 * u, 4), :] = g_ref[
+                pl.ds(pl.multiple_of(4 * c, 4), 4), :
+            ]
+
+    @pl.loop(0, owners // 16)
+    def _(i):
+        for u in range(16):
+            o = i * 16 + u
+            o_ref[o] = f_ref[pl.ds(pl.multiple_of(o * PER, PER), PER), :].astype(BF)
+
+
+def plane_pass(received, volume, tabs):
     owners = received.shape[0]
     return pl.pallas_call(
         plane_kernel,
         out_shape=jax.ShapeDtypeStruct((owners, PER, LANES), BF),
-        in_specs=[SMEM, VMEM] + [HBM] * 5,
+        in_specs=[VMEM] + [HBM] * 5,
         out_specs=VMEM,
         scratch_shapes=[
             pltpu.VMEM(volume.shape, F32),
@@ -276,14 +280,16 @@
             pltpu.VMEM((SIDE * BOX * 4, LANES), F32),
             pltpu.VMEM((2, 2 * NR * STEP, LANES), F32),
             pltpu.VMEM((32, 2 * NR, 2 * LANES), BF),
-            pltpu.SemaphoreType.DMA((5,)),
+            pltpu.VMEM((owners, LANES), jnp.int32),
+            pltpu.SMEM((owners, LANES), jnp.int32),
+            pltpu.SemaphoreType.DMA((6,)),
         ],
         compiler_params=pltpu.CompilerParams(vmem_limit_bytes=48 << 20),
         cost_estimate=pl.CostEstimate(
             flops=2 * 77000 * 256 * 256, bytes_accessed=6 << 20, transcendentals=0
         ),
         name="plane",
-    )(cells, received, volume, *tabs)
+    )(received, volume, *tabs)
 
 
 def finish_kernel(r_ref, place_ref, i_ref, o_hbm, t_ref, sp_ref, out_ref, sem):
@@ -352,10 +358,8 @@
     place = g_place.reshape(1, -1)
     sent = spread(coeffs, place, stick_column, ahead_x)
     got = exchange(sent)
-    column = got[:, PER, : 2 * SLOT].astype(F32).astype(jnp.int32)
-    cells = (column[:, :SLOT] * BOX + column[:, SLOT:]).reshape(-1)
     volume = potential.reshape(NR, NR)
-    done = plane_pass(cells, got, volume, (ahead_y, ahead_x, behind_x, behind_y))
+    done = plane_pass(got, volume, (ahead_y, ahead_x, behind_x, behind_y))
     return finish(exchange(done), place, behind_x)
 
 

time: 104 us -> 105 us (level)
  Pallas kernels: 25.1 us -> 26.4 us
    pallas_call x1, Pallas kernels: 18.6 us -> 19.9 us  [plane_pass(): pl.pallas_call(plane_kernel, out_shape=jax.ShapeDtypeStruct((owners, PER,...]
where the time goes in v5:
time: 105 us
  blocking collectives  78.3 us (75%)
  Pallas kernels  26.4 us (25%)
    all_to_all x2, blocking collectives, exchange(): return lax.all_to_all(value, TG_PW, split_axis=0, concat_axis=0, tiled=True)  78.3 us
    pallas_call x1, Pallas kernels, plane_pass(): pl.pallas_call(plane_kernel, out_shape=jax.ShapeDtypeStruct((owners, PER,...  19.9 us
    pallas_call x1, Pallas kernels, spread(): pl.pallas_call(spread_kernel, out_shape=out, in_specs=[HBM, HBM, SMEM, HB...  4.28 us
    pallas_call x1, Pallas kernels, finish(): pl.pallas_call(finish_kernel, out_shape=out, in_specs=[VMEM] * 3, out_spe...  2.16 us

profile of v5, /device:TPU:1, one launch (start us, length us, event | category | flops | bytes accessed | tf_op | source)
XLA Modules:
  0.0 104.8 jit_solution(9574643373282194249)
XLA Ops:
  0.0 4.3 %spread.1 = bf16[128,72,128]{2,1,0:T(8,128)(2,1)} custom-call(f32[2,256,256]{2,1,0:T(8,128)} %c_hbm.1, s32[1,256]{1,0:T(1,128)} %bitcast.2, s32[16]{0:T(128)} %column_ref.1, bf16[256,144]{1,0:T(8,128)(2,1)} %constant.8.clone.e_hbm.ex_hbm), custom_call_target="tpu_custom_call" | custom-call | flops 838860800 | bytes 3145728 | tf_op jit(solution)/shard_map/spread/pallas_call | solution.py:111
  4.3 0.0 copy-start
  4.3 0.0 copy-start.2
  4.3 0.0 copy-start.3
  4.3 0.0 copy-start.4
  4.3 0.0 copy-start.5
  4.3 42.9 %all_to_all.10.r_in = bf16[128,72,128]{2,1,0:T(8,128)(2,1)S(1)} all-to-all(bf16[128,72,128]{2,1,0:T(8,128)(2,1)} %spread.1), channel_id=1, replica_groups=mesh['tg'=2,'pw_0'=4,'pw_1'=4,'pw_2'=4] {'tg','pw_0','pw_1','pw_2'}, dimensions={0} | all-to-all | bytes 4718592 | tf_op jit(solution)/shard_map/all_to_all | solution.py:353
  47.2 0.0 copy-done
  47.2 0.0 copy-done.2
  47.2 0.0 copy-done.3
  47.2 0.0 copy-done.4
  47.2 0.0 copy-done.5
  47.2 19.9 %plane.1 = bf16[128,64,128]{2,1,0:T(8,128)(2,1)S(1)} custom-call(bf16[128,72,128]{2,1,0:T(8,128)(2,1)S(1)} %all_to_all.10.r_in, f32[128,128]{1,0:T(8,128)S(1)} %bitcast.4, bf16[256,144]{1,0:T(8,128)(2,1)S(1)} %copy-done.4, bf16[256,144]{1,0:T(8,128)(2,1)S(1)} %copy-done.3, bf16[144,256]{1,0:T(8,128)(2,1)S(1)} %copy-done, bf16[144,256]{1,0:T(8,128)(2,1)S(1)} %copy-done.5), custom_call_target="tpu_custom_call" | custom-call | flops 10092544000 | bytes 6291456 | tf_op jit(solution)/shard_map/plane/pallas_call | solution.py:271
  67.2 0.0 copy-start.1
  67.2 35.4 %all_to_all.11.r_ref = bf16[128,64,128]{2,1,0:T(8,128)(2,1)S(1)} all-to-all(bf16[128,64,128]{2,1,0:T(8,128)(2,1)S(1)} %plane.1), channel_id=1, replica_groups=mesh['tg'=2,'pw_0'=4,'pw_1'=4,'pw_2'=4] {'tg','pw_0','pw_1','pw_2'}, dimensions={0} | all-to-all | bytes 4194304 | tf_op jit(solution)/shard_map/all_to_all | solution.py:353
  102.6 0.0 copy-done.1
  102.6 2.2 %finish.1 = f32[2,256,256]{2,1,0:T(8,128)} custom-call(bf16[128,64,128]{2,1,0:T(8,128)(2,1)S(1)} %all_to_all.11.r_ref, s32[1,256]{1,0:T(1,128)S(1)} %bitcast.3, bf16[144,256]{1,0:T(8,128)(2,1)S(1)} %copy-done), custom_call_target="tpu_custom_call" | custom-call | flops 637534208 | bytes 3145728 | tf_op jit(solution)/shard_map/finish/pallas_call | solution.py:333
Async XLA Ops:
  4.3 42.9 %copy-start = (bf16[144,256]{1,0:T(8,128)(2,1)S(1)}, bf16[144,256]{1,0:T(8,128)(2,1)}, u32[]{:S(2)}) copy-start(bf16[144,256]{1,0:T(8,128)(2,1)} %constant.9.clone.ix_hbm.i_ref) | copy-start | bytes 221188
  4.3 42.9 %copy-start.2 = (f32[128,128,1]{1,2,0:T(1,128)S(1)}, f32[128,128,1]{1,2,0:T(1,128)}, u32[]{:S(2)}) copy-start(f32[128,128,1]{1,2,0:T(1,128)} %param.11) | copy-start | bytes 196612
  4.3 42.9 %copy-start.3 = (bf16[256,144]{1,0:T(8,128)(2,1)S(1)}, bf16[256,144]{1,0:T(8,128)(2,1)}, u32[]{:S(2)}) copy-start(bf16[256,144]{1,0:T(8,128)(2,1)} %constant.8.clone.e_hbm.ex_hbm) | copy-start | bytes 221188
  4.3 42.9 %copy-start.4 = (bf16[256,144]{1,0:T(8,128)(2,1)S(1)}, bf16[256,144]{1,0:T(8,128)(2,1)}, u32[]{:S(2)}) copy-start(bf16[256,144]{1,0:T(8,128)(2,1)} %constant.11.clone.ey_hbm) | copy-start | bytes 221188
  4.3 42.9 %copy-start.5 = (bf16[144,256]{1,0:T(8,128)(2,1)S(1)}, bf16[144,256]{1,0:T(8,128)(2,1)}, u32[]{:S(2)}) copy-start(bf16[144,256]{1,0:T(8,128)(2,1)} %constant.10.clone.iy_hbm) | copy-start | bytes 221188
  67.2 35.4 %copy-start.1 = (s32[256]{0:T(256)S(1)}, s32[256]{0:T(256)}, u32[]{:S(2)}) copy-start(s32[256]{0:T(256)} %param.9) | copy-start | bytes 3076

commit v6 on v4

--- a/solution.py
+++ b/solution.py
@@ -171,7 +171,7 @@
         def _(i):
             for u in range(step):
                 c = cell_ref[i * step + u]
-                g_ref[pl.ds(pl.multiple_of(4 * c, 4), 4), :] = f_ref[
+                g_ref[pl.ds(pl.multiple_of(c, 4), 4), :] = f_ref[
                     pl.ds(pl.multiple_of(i * 4 * step, 4 * step) + 4 * u, 4), :
                 ]
 
@@ -252,7 +252,7 @@
             for u in range(step):
                 c = cell_ref[i * step + u]
                 f_ref[pl.ds(pl.multiple_of(i * 4 * step, 4 * step) + 4 * u, 4), :] = g_ref[
-                    pl.ds(pl.multiple_of(4 * c, 4), 4), :
+                    pl.ds(pl.multiple_of(c, 4), 4), :
                 ]
 
         @pl.loop(q * share // 16, (q + 1) * share // 16)
@@ -353,7 +353,7 @@
     sent = spread(coeffs, place, stick_column, ahead_x)
     got = exchange(sent)
     column = got[:, PER, : 2 * SLOT].astype(F32).astype(jnp.int32)
-    cells = (column[:, :SLOT] * BOX + column[:, SLOT:]).reshape(-1)
+    cells = (column[:, :SLOT] * (4 * BOX) + column[:, SLOT:] * 4).reshape(-1)
     volume = potential.reshape(NR, NR)
     done = plane_pass(cells, got, volume, (ahead_y, ahead_x, behind_x, behind_y))
     return finish(exchange(done), place, behind_x)

time: 104 us -> 103 us (level)
  Pallas kernels: 25.1 us -> 24 us
    pallas_call x1, Pallas kernels: 18.6 us -> 17.6 us  [plane_pass(): pl.pallas_call(plane_kernel, out_shape=jax.ShapeDtypeStruct((owners, PER,...]
where the time goes in v6:
time: 103 us
  blocking collectives  78.3 us (76%)
  Pallas kernels  24 us (23%)
    all_to_all x2, blocking collectives, exchange(): return lax.all_to_all(value, TG_PW, split_axis=0, concat_axis=0, tiled=True)  78.3 us
    pallas_call x1, Pallas kernels, plane_pass(): pl.pallas_call(plane_kernel, out_shape=jax.ShapeDtypeStruct((owners, PER,...  17.6 us
    pallas_call x1, Pallas kernels, spread(): pl.pallas_call(spread_kernel, out_shape=out, in_specs=[HBM, HBM, SMEM, HB...  4.28 us
    pallas_call x1, Pallas kernels, finish(): pl.pallas_call(finish_kernel, out_shape=out, in_specs=[VMEM] * 3, out_spe...  2.16 us

profile of v6, /device:TPU:1, one launch (start us, length us, event | category | flops | bytes accessed | tf_op | source)
XLA Modules:
  0.0 102.6 jit_solution(17141645384867840499)
XLA Ops:
  0.0 4.3 %spread.1 = bf16[128,72,128]{2,1,0:T(8,128)(2,1)} custom-call(f32[2,256,256]{2,1,0:T(8,128)} %c_hbm.1, s32[1,256]{1,0:T(1,128)} %bitcast.3, s32[16]{0:T(128)} %column_ref.1, bf16[256,144]{1,0:T(8,128)(2,1)} %constant.12.clone.e_hbm.ex_hbm), custom_call_target="tpu_custom_call" | custom-call | flops 838860800 | bytes 3145728 | tf_op jit(solution)/shard_map/spread/pallas_call | solution.py:111
  4.3 0.0 copy-start
  4.3 0.0 copy-start.2
  4.3 0.0 copy-start.3
  4.3 0.0 copy-start.4
  4.3 0.0 copy-start.5
  4.3 42.9 %all_to_all.10.r_in = bf16[128,72,128]{2,1,0:T(8,128)(2,1)S(1)} all-to-all(bf16[128,72,128]{2,1,0:T(8,128)(2,1)} %spread.1), channel_id=1, replica_groups=mesh['tg'=2,'pw_0'=4,'pw_1'=4,'pw_2'=4] {'tg','pw_0','pw_1','pw_2'}, dimensions={0} | all-to-all | bytes 4718592 | tf_op jit(solution)/shard_map/all_to_all | solution.py:347
  47.2 0.1 fusion.1
  47.3 0.1 fusion
  47.4 0.1 reshape.12.cell_ref
  47.4 0.0 copy-done
  47.4 0.0 copy-done.2
  47.5 0.0 copy-done.3
  47.5 0.0 copy-done.4
  47.5 0.0 copy-done.5
  47.5 17.6 %plane.1 = bf16[128,64,128]{2,1,0:T(8,128)(2,1)S(1)} custom-call(s32[2048]{0:T(1024)S(1)} %reshape.12.cell_ref, bf16[128,72,128]{2,1,0:T(8,128)(2,1)S(1)} %all_to_all.10.r_in, f32[128,128]{1,0:T(8,128)S(1)} %bitcast.5, bf16[256,144]{1,0:T(8,128)(2,1)S(1)} %copy-done.4, bf16[256,144]{1,0:T(8,128)(2,1)S(1)} %copy-done.3, bf16[144,256]{1,0:T(8,128)(2,1)S(1)} %copy-done, ...), custom_call_target="tpu_custom_call" | custom-call | flops 10092544000 | bytes 6291456 | tf_op jit(solution)/shard_map/plane/pallas_call | solution.py:267
  65.1 0.0 copy-start.1
  65.1 35.4 %all_to_all.11.r_ref = bf16[128,64,128]{2,1,0:T(8,128)(2,1)S(1)} all-to-all(bf16[128,64,128]{2,1,0:T(8,128)(2,1)S(1)} %plane.1), channel_id=1, replica_groups=mesh['tg'=2,'pw_0'=4,'pw_1'=4,'pw_2'=4] {'tg','pw_0','pw_1','pw_2'}, dimensions={0} | all-to-all | bytes 4194304 | tf_op jit(solution)/shard_map/all_to_all | solution.py:347
  100.5 0.0 copy-done.1
  100.5 2.2 %finish.1 = f32[2,256,256]{2,1,0:T(8,128)} custom-call(bf16[128,64,128]{2,1,0:T(8,128)(2,1)S(1)} %all_to_all.11.r_ref, s32[1,256]{1,0:T(1,128)S(1)} %bitcast.4, bf16[144,256]{1,0:T(8,128)(2,1)S(1)} %copy-done), custom_call_target="tpu_custom_call" | custom-call | flops 637534208 | bytes 3145728 | tf_op jit(solution)/shard_map/finish/pallas_call | solution.py:327
Async XLA Ops:
  4.3 43.2 %copy-start = (bf16[144,256]{1,0:T(8,128)(2,1)S(1)}, bf16[144,256]{1,0:T(8,128)(2,1)}, u32[]{:S(2)}) copy-start(bf16[144,256]{1,0:T(8,128)(2,1)} %constant.13.clone.ix_hbm.i_ref) | copy-start | bytes 221188
  4.3 43.1 %copy-start.2 = (f32[128,128,1]{1,2,0:T(1,128)S(1)}, f32[128,128,1]{1,2,0:T(1,128)}, u32[]{:S(2)}) copy-start(f32[128,128,1]{1,2,0:T(1,128)} %param.11) | copy-start | bytes 196612
  4.3 43.1 %copy-start.3 = (bf16[256,144]{1,0:T(8,128)(2,1)S(1)}, bf16[256,144]{1,0:T(8,128)(2,1)}, u32[]{:S(2)}) copy-start(bf16[256,144]{1,0:T(8,128)(2,1)} %constant.12.clone.e_hbm.ex_hbm) | copy-start | bytes 221188
  4.3 43.1 %copy-start.4 = (bf16[256,144]{1,0:T(8,128)(2,1)S(1)}, bf16[256,144]{1,0:T(8,128)(2,1)}, u32[]{:S(2)}) copy-start(bf16[256,144]{1,0:T(8,128)(2,1)} %constant.15.clone.ey_hbm) | copy-start | bytes 221188
  4.3 43.1 %copy-start.5 = (bf16[144,256]{1,0:T(8,128)(2,1)S(1)}, bf16[144,256]{1,0:T(8,128)(2,1)}, u32[]{:S(2)}) copy-start(bf16[144,256]{1,0:T(8,128)(2,1)} %constant.14.clone.iy_hbm) | copy-start | bytes 221188
  65.1 35.4 %copy-start.1 = (s32[256]{0:T(256)S(1)}, s32[256]{0:T(256)}, u32[]{:S(2)}) copy-start(s32[256]{0:T(256)} %param.9) | copy-start | bytes 3076
